TPU v7x, 32 devices: a whole 2x2x4 slice. The times are simulated.
32 devices in a mesh: groups: 2 (over y), frame: 4 (over z), space: 4 (over x, core).
Axes of the slice: x: 2, y: 2, z: 4, core: 2. Of those that a mesh axis runs over, the one named last changes fastest.
Arguments:
- queries: float32 [16384, 128], P(('groups', 'frame', 'space')), parts along dimension 0, may hold values from -256 to 256
- keys: float32 [16384, 128], P(('groups', 'frame', 'space')), parts along dimension 0, may hold values from -8 to 8
- values: float32 [16384, 128], P(('groups', 'frame', 'space')), parts along dimension 0, may hold values from -6 to 6
- block_mask: int32 [4, 4], replicated, may hold values from 0 to 1, as said below
- partner_flags: int32 [4, 2, 2], replicated, may hold values 0 or 1
Outputs:
- attended: float32 [16384, 128], P(('groups', 'frame', 'space')), parts along dimension 0
There are 2 independent parts, one for each index of `groups`. A program takes and returns all parts, laid end to end along the dimension named above; an argument that names none is the same for every part. Nothing has to cross between parts.
Inputs may be any that keep to these rules, and one draw needn't show every extreme that they name: block_mask[a, b] = 1 when a = b or |a - b| = 2, and block_mask[a, b] = 0 when |a - b| > 2. `partner_flags`: a partner outside frame groups 0 to 3 is never used, whatever its flag.
All inputs are finite; a program needn't handle non-finite values.
Results may differ from a plain program's by a relative error of at most 0.0003.
Values sent between devices are 32-bit elements; how exact they have to be, the bound alone decides.
No kernel may reach another device: no remote copies, remote signals or barrier semaphores. Data moves between devices by JAX's collectives and lax.ppermute only.
A program may use at most 64 MiB of HBM per device.

v0:
```python
import math

import jax
import jax.numpy as jnp
from jax import lax
from jax.sharding import PartitionSpec as P

masked_score = -1e30


def shifted(block, axis, distance):
    devices = range(lax.axis_size(axis))
    route = [(i - distance, i) for i in devices if i - distance in devices]
    return lax.ppermute(block, axis, route)


def score_block(query_rows, key_rows):
    return lax.dot_general(
        query_rows,
        key_rows,
        (((1,), (1,)), ((), ())),
        precision=lax.Precision.HIGHEST,
        preferred_element_type=jnp.float32,
    )


def absorb(state, query_rows, key_rows, value_rows, allowed):
    row_count, head_width = key_rows.shape
    block_rows = 512
    block_count = row_count // block_rows
    score_scale = 1.0 / math.sqrt(head_width)

    def absorb_block(carried, pieces):
        key_block, value_block, allowed_block = pieces
        running_max, row_total, weighted = carried
        scores = score_block(query_rows, key_block) * score_scale
        scores = jnp.where(allowed_block[None, :], scores, masked_score)
        new_max = jnp.maximum(running_max, jnp.max(scores, axis=1))
        weights = jnp.where(allowed_block[None, :], jnp.exp(scores - new_max[:, None]), 0.0)
        factor = jnp.exp(running_max - new_max)
        row_total = row_total * factor + jnp.sum(weights, axis=1)
        weighted = weighted * factor[:, None] + jnp.dot(
            weights,
            value_block,
            precision=lax.Precision.HIGHEST,
            preferred_element_type=jnp.float32,
        )
        return ((new_max, row_total, weighted), None)

    carried, _ = lax.scan(
        absorb_block,
        state,
        (
            key_rows.reshape(block_count, block_rows, head_width),
            value_rows.reshape(block_count, block_rows, head_width),
            allowed.reshape(block_count, block_rows),
        ),
    )
    return carried


def per_device(queries, keys, values, block_mask, partner_flags):
    tok_rows, head_width = queries.shape
    blocks = lax.axis_size("space")
    groups = lax.axis_size("frame")
    levels = groups.bit_length() - 1
    space_index = lax.axis_index("space")
    group_index = lax.axis_index("frame")
    own_row = lax.dynamic_index_in_dim(block_mask, space_index, 0, keepdims=False)
    flag_rows = lax.dynamic_index_in_dim(partner_flags, group_index, 0, keepdims=False)
    far_keys = []
    far_values = []
    far_allowed = []
    for level_index in range(levels):
        distance = 2**level_index
        for direction in range(2):
            offset = distance if direction == 0 else -distance
            moved_keys, moved_values = shifted((keys, values), "frame", offset)
            partner = group_index - offset
            usable = (partner >= 0) & (partner < groups) & (flag_rows[level_index, direction] > 0)
            far_keys.append(moved_keys)
            far_values.append(moved_values)
            far_allowed.append(jnp.broadcast_to(usable, (tok_rows,)))
    initial = (
        jnp.full((tok_rows,), masked_score, jnp.float32),
        jnp.zeros((tok_rows,), jnp.float32),
        jnp.zeros((tok_rows, head_width), jnp.float32),
    )
    state = absorb(
        initial,
        queries,
        jnp.concatenate(far_keys, axis=0),
        jnp.concatenate(far_values, axis=0),
        jnp.concatenate(far_allowed, axis=0),
    )
    key_piece = lax.all_gather(keys, "space", axis=0, tiled=True)
    value_piece = lax.all_gather(values, "space", axis=0, tiled=True)
    row_count = key_piece.shape[0]
    owner = lax.broadcasted_iota(jnp.int32, (row_count,), 0) // tok_rows
    matched = owner[:, None] == lax.broadcasted_iota(jnp.int32, (1, blocks), 1)
    allowed = jnp.any(matched & (own_row[None, :] > 0), axis=1)
    state = absorb(state, queries, key_piece, value_piece, allowed)
    running_max, row_total, weighted = state
    return weighted / row_total[:, None]


def solution(mesh):
    in_specs = (
        P(("groups", "frame", "space"), None),
        P(("groups", "frame", "space"), None),
        P(("groups", "frame", "space"), None),
        P(),
        P(),
    )
    out_specs = P(("groups", "frame", "space"), None)
    return jax.shard_map(
        per_device, mesh=mesh, in_specs=in_specs, out_specs=out_specs, check_vma=False
    )
```

profile of v0, /device:TPU:0, one launch (start us, length us, event | category | flops | bytes accessed | tf_op | source)
XLA Modules:
  0.0 99.6 jit_solution(3641384196366600638)
XLA Ops:
  6.5 0.7 all-gather.5.cloned.1.call-update
  7.3 0.0 all-gather.3.cloned.1.call-start
  7.3 5.0 %collective-permute-start = (f32[512,128]{1,0:T(8,128)}, f32[512,128]{1,0:T(8,128)S(1)}, u32[]{:S(2)}, u32[]{:S(2)}) collective-permute-start(f32[512,128]{1,0:T(8,128)} %param.10), channel_id=1, source_target_pairs={{0,4},{4,8},{8,12},{1,5},{5,9},{9,13},{2,6},{6,10},{10,14},{3,7},{... | collective-permute-start | bytes 786440 | tf_op jit(solution)/shard_map/ppermute | solution.py:14
  12.3 1.3 %collective-permute-start.1 = (f32[512,128]{1,0:T(8,128)}, f32[512,128]{1,0:T(8,128)S(1)}, u32[]{:S(2)}, u32[]{:S(2)}) collective-permute-start(f32[512,128]{1,0:T(8,128)} %param.10), channel_id=1, source_target_pairs={{4,0},{8,4},{12,8},{5,1},{9,5},{13,9},{6,2},{10,6},{14,10},{7,3},{... | collective-permute-start | bytes 786440 | tf_op jit(solution)/shard_map/ppermute | solution.py:14
  13.6 5.6 %collective-permute-start.2 = (f32[512,128]{1,0:T(8,128)}, f32[512,128]{1,0:T(8,128)S(1)}, u32[]{:S(2)}, u32[]{:S(2)}) collective-permute-start(f32[512,128]{1,0:T(8,128)} %param.10), channel_id=1, source_target_pairs={{0,8},{4,12},{1,9},{5,13},{2,10},{6,14},{3,11},{7,15},{16,24},{20,... | collective-permute-start | bytes 786440 | tf_op jit(solution)/shard_map/ppermute | solution.py:14
  19.2 1.3 %collective-permute-start.3 = (f32[512,128]{1,0:T(8,128)}, f32[512,128]{1,0:T(8,128)S(1)}, u32[]{:S(2)}, u32[]{:S(2)}) collective-permute-start(f32[512,128]{1,0:T(8,128)} %param.10), channel_id=1, source_target_pairs={{8,0},{12,4},{9,1},{13,5},{10,2},{14,6},{11,3},{15,7},{24,16},{28,... | collective-permute-start | bytes 786440 | tf_op jit(solution)/shard_map/ppermute | solution.py:14
  20.5 3.5 %collective-permute-start.4 = (f32[512,128]{1,0:T(8,128)S(1)}, f32[512,128]{1,0:T(8,128)S(1)}, u32[]{:S(2)}, u32[]{:S(2)}) collective-permute-start(f32[512,128]{1,0:T(8,128)S(1)} %copy-done.2), channel_id=1, source_target_pairs={{0,4},{4,8},{8,12},{1,5},{5,9},{9,13},{2,6},{6,10},{10,14},{3,7},{... | collective-permute-start | bytes 786440 | tf_op jit(solution)/shard_map/ppermute | solution.py:14
  24.0 0.0 all-gather.3.cloned.1.call-update
  24.0 0.2 dynamic-slice_reduce_fusion.2
  24.2 0.6 fusion.32
  24.9 0.7 compare_bitcast_fusion
  28.0 0.1 fusion.26
  28.1 1.3 %collective-permute-start.5 = (f32[512,128]{1,0:T(8,128)S(1)}, f32[512,128]{1,0:T(8,128)S(1)}, u32[]{:S(2)}, u32[]{:S(2)}) collective-permute-start(f32[512,128]{1,0:T(8,128)S(1)} %copy-done.2), channel_id=1, source_target_pairs={{4,0},{8,4},{12,8},{5,1},{9,5},{13,9},{6,2},{10,6},{14,10},{7,3},{... | collective-permute-start | bytes 786440 | tf_op jit(solution)/shard_map/ppermute | solution.py:14
  29.4 6.5 %collective-permute-start.6 = (f32[512,128]{1,0:T(8,128)S(1)}, f32[512,128]{1,0:T(8,128)S(1)}, u32[]{:S(2)}, u32[]{:S(2)}) collective-permute-start(f32[512,128]{1,0:T(8,128)S(1)} %copy-done.2), channel_id=1, source_target_pairs={{0,8},{4,12},{1,9},{5,13},{2,10},{6,14},{3,11},{7,15},{16,24},{20,... | collective-permute-start | bytes 786440 | tf_op jit(solution)/shard_map/ppermute | solution.py:14
  35.9 1.3 %collective-permute-start.7 = (f32[512,128]{1,0:T(8,128)S(1)}, f32[512,128]{1,0:T(8,128)}, u32[]{:S(2)}, u32[]{:S(2)}) collective-permute-start(f32[512,128]{1,0:T(8,128)S(1)} %copy-done.2), channel_id=1, source_target_pairs={{8,0},{12,4},{9,1},{13,5},{10,2},{14,6},{11,3},{15,7},{24,16},{28,... | collective-permute-start | bytes 786440 | tf_op jit(solution)/shard_map/ppermute | solution.py:14
  37.4 0.1 pad_maximum_fusion
  37.5 3.5 %collective-permute-done.5 = f32[512,128]{1,0:T(8,128)S(1)} collective-permute-done((f32[512,128]{1,0:T(8,128)S(1)}, f32[512,128]{1,0:T(8,128)S(1)}, u32[]{:S(2)}, u32[]{:S(2)}) %collective-permute-start.5) | collective-permute-done | bytes 262176 | tf_op jit(solution)/shard_map/ppermute | solution.py:14
  41.0 11.0 %collective-permute-done.7 = f32[512,128]{1,0:T(8,128)} collective-permute-done((f32[512,128]{1,0:T(8,128)S(1)}, f32[512,128]{1,0:T(8,128)}, u32[]{:S(2)}, u32[]{:S(2)}) %collective-permute-start.7) | collective-permute-done | bytes 262176 | tf_op jit(solution)/shard_map/ppermute | solution.py:14
  52.0 2.0 %pad_maximum_fusion.1 = f32[2048,128]{1,0:T(8,128)} fusion(f32[512,128]{1,0:T(8,128)} %collective-permute-done.7, f32[512,128]{1,0:T(8,128)S(1)} %collective-permute-done.6, f32[512,128]{1,0:T(8,128)S(1)} %collective-permute-done.5, f32[512,128]{1,0:T(8,128)S(1)} %collective-permute-done.4), kind=kLoop, calls=%fused_computation.40 | loop fusion | flops 786432 | bytes 2097152 | tf_op jit(solution)/shard_map/concatenate | solution.py:93
  54.0 17.0 %while.30 = (s32[]{:T(128)}, f32[512]{0:T(512)S(1)}, f32[512]{0:T(512)S(1)}, f32[512,128]{1,0:T(8,128)S(1)}, pred[4,512]{1,0:T(4,128)(4,1)S(1)}, /*index=5*/f32[...) while((s32[]{:T(128)}, f32[512]{0:T(512)S(1)}, ...), condition=%wide.region_3.4_spmd.clone, body=%wide.region_0.3_spmd.clone.sunk | while | flops 807602688 | bytes 4492409 | solution.py:50
  54.0 1.1 %fusion.50 = (f32[512]{0:T(512)S(1)}, f32[512,512]{1,0:T(8,128)S(1)}) fusion(f32[512,128]{1,0:T(8,128)S(1)} %get-tuple-element.308, f32[4,512,128]{2,1,0:T(8,128)S(1)} %get-tuple-element.307, s32[]{:T(128)} %get-tuple-element.292, pred[512]{0:T(512)(128)(4,1)S(1)} %dynamic-slice_reduce_fusion.6), kind=kOutput, calls=%fused_computation.56.clone.1 | convolution fusion | flops 403439104 | bytes 1575428 | tf_op jit(solution)/shard_map/while/body/eval_jaxpr/dot_general | solution.py:18
  55.1 0.2 fusion.51
  55.3 2.9 %convolution_add_fusion.5 = f32[512,128]{1,0:T(8,128)S(1)} fusion(f32[512,512]{1,0:T(8,128)S(1)} %get-tuple-element.279, f32[512]{0:T(512)S(1)} %select_maximum_fusion.2, pred[512]{0:T(512)(128)(4,1)S(1)} %dynamic-slice_reduce_fusion.6, f32[512,128]{1,0:T(8,128)S(1)} %get-tuple-element.295, f32[4,512,128]{2,1,0:T(8,128)} %get-tuple-element.309, ...), kind=kOutput, calls=%fused_computation.20.clone.1 | convolution fusion | flops 403374080 | bytes 1840129 | tf_op jit(solution)/shard_map/while/body/eval_jaxpr/dot_general | solution.py:42
  58.3 1.0 %fusion.50 = (f32[512]{0:T(512)S(1)}, f32[512,512]{1,0:T(8,128)S(1)}) fusion(f32[512,128]{1,0:T(8,128)S(1)} %get-tuple-element.308, f32[4,512,128]{2,1,0:T(8,128)S(1)} %get-tuple-element.307, s32[]{:T(128)} %get-tuple-element.292, pred[512]{0:T(512)(128)(4,1)S(1)} %dynamic-slice_reduce_fusion.6), kind=kOutput, calls=%fused_computation.56.clone.1 | convolution fusion | flops 403439104 | bytes 1575428 | tf_op jit(solution)/shard_map/while/body/eval_jaxpr/dot_general | solution.py:18
  59.4 0.2 fusion.51
  59.6 2.9 %convolution_add_fusion.5 = f32[512,128]{1,0:T(8,128)S(1)} fusion(f32[512,512]{1,0:T(8,128)S(1)} %get-tuple-element.279, f32[512]{0:T(512)S(1)} %select_maximum_fusion.2, pred[512]{0:T(512)(128)(4,1)S(1)} %dynamic-slice_reduce_fusion.6, f32[512,128]{1,0:T(8,128)S(1)} %get-tuple-element.295, f32[4,512,128]{2,1,0:T(8,128)} %get-tuple-element.309, ...), kind=kOutput, calls=%fused_computation.20.clone.1 | convolution fusion | flops 403374080 | bytes 1840129 | tf_op jit(solution)/shard_map/while/body/eval_jaxpr/dot_general | solution.py:42
  62.5 1.0 %fusion.50 = (f32[512]{0:T(512)S(1)}, f32[512,512]{1,0:T(8,128)S(1)}) fusion(f32[512,128]{1,0:T(8,128)S(1)} %get-tuple-element.308, f32[4,512,128]{2,1,0:T(8,128)S(1)} %get-tuple-element.307, s32[]{:T(128)} %get-tuple-element.292, pred[512]{0:T(512)(128)(4,1)S(1)} %dynamic-slice_reduce_fusion.6), kind=kOutput, calls=%fused_computation.56.clone.1 | convolution fusion | flops 403439104 | bytes 1575428 | tf_op jit(solution)/shard_map/while/body/eval_jaxpr/dot_general | solution.py:18
  63.6 0.2 fusion.51
  63.8 2.9 %convolution_add_fusion.5 = f32[512,128]{1,0:T(8,128)S(1)} fusion(f32[512,512]{1,0:T(8,128)S(1)} %get-tuple-element.279, f32[512]{0:T(512)S(1)} %select_maximum_fusion.2, pred[512]{0:T(512)(128)(4,1)S(1)} %dynamic-slice_reduce_fusion.6, f32[512,128]{1,0:T(8,128)S(1)} %get-tuple-element.295, f32[4,512,128]{2,1,0:T(8,128)} %get-tuple-element.309, ...), kind=kOutput, calls=%fused_computation.20.clone.1 | convolution fusion | flops 403374080 | bytes 1840129 | tf_op jit(solution)/shard_map/while/body/eval_jaxpr/dot_general | solution.py:42
  66.8 1.0 %fusion.50 = (f32[512]{0:T(512)S(1)}, f32[512,512]{1,0:T(8,128)S(1)}) fusion(f32[512,128]{1,0:T(8,128)S(1)} %get-tuple-element.308, f32[4,512,128]{2,1,0:T(8,128)S(1)} %get-tuple-element.307, s32[]{:T(128)} %get-tuple-element.292, pred[512]{0:T(512)(128)(4,1)S(1)} %dynamic-slice_reduce_fusion.6), kind=kOutput, calls=%fused_computation.56.clone.1 | convolution fusion | flops 403439104 | bytes 1575428 | tf_op jit(solution)/shard_map/while/body/eval_jaxpr/dot_general | solution.py:18
  67.9 0.2 fusion.51
  68.1 2.9 %convolution_add_fusion.5 = f32[512,128]{1,0:T(8,128)S(1)} fusion(f32[512,512]{1,0:T(8,128)S(1)} %get-tuple-element.279, f32[512]{0:T(512)S(1)} %select_maximum_fusion.2, pred[512]{0:T(512)(128)(4,1)S(1)} %dynamic-slice_reduce_fusion.6, f32[512,128]{1,0:T(8,128)S(1)} %get-tuple-element.295, f32[4,512,128]{2,1,0:T(8,128)} %get-tuple-element.309, ...), kind=kOutput, calls=%fused_computation.20.clone.1 | convolution fusion | flops 403374080 | bytes 1840129 | tf_op jit(solution)/shard_map/while/body/eval_jaxpr/dot_general | solution.py:42
  71.0 0.0 all-gather.5.cloned.1.call-done
  71.1 0.0 all-gather.3.cloned.1.call-done
  71.1 20.8 %while.29 = (s32[]{:T(128)}, f32[512]{0:T(512)S(1)}, f32[512]{0:T(512)S(1)}, f32[512,128]{1,0:T(8,128)S(1)}, pred[4,512]{1,0:T(4,128)(4,1)S(1)}, /*index=5*/f32[...) while((s32[]{:T(128)}, f32[512]{0:T(512)S(1)}, f32[512]{0:T(512)S(1)}, ...), condition=%wide.region_8.9_spmd, body=%wide.region_5.8_spmd.sunk | while | flops 807535616 | bytes 4492897 | solution.py:50
  71.1 2.0 %fusion.46 = (f32[512]{0:T(512)S(1)}, f32[512,512]{1,0:T(8,128)S(1)}) fusion(f32[512,128]{1,0:T(8,128)S(1)} %get-tuple-element.336, f32[4,512,128]{2,1,0:T(8,128)} %get-tuple-element.335, s32[]{:T(128)} %get-tuple-element.321, pred[512]{0:T(512)(128)(4,1)S(1)} %dynamic-slice_reduce_fusion.5), kind=kOutput, calls=%fused_computation.55.clone.1 | convolution fusion | flops 403439104 | bytes 1575936 | tf_op jit(solution)/shard_map/while/body/eval_jaxpr/dot_general | solution.py:18
  73.1 0.2 fusion.47
  73.4 2.9 %convolution_add_fusion.4 = f32[512,128]{1,0:T(8,128)S(1)} fusion(f32[512,512]{1,0:T(8,128)S(1)} %get-tuple-element.267, f32[512]{0:T(512)S(1)} %max.10, pred[512]{0:T(512)(128)(4,1)S(1)} %dynamic-slice_reduce_fusion.5, f32[4,512,128]{2,1,0:T(8,128)} %get-tuple-element.337, s32[]{:T(128)} %get-tuple-element.321, ...), kind=kOutput, calls=%fused_computation.2.clone.1 | convolution fusion | flops 403308544 | bytes 1840128 | tf_op jit(solution)/shard_map/while/body/eval_jaxpr/dot_general | solution.py:42
  76.3 2.0 %fusion.46 = (f32[512]{0:T(512)S(1)}, f32[512,512]{1,0:T(8,128)S(1)}) fusion(f32[512,128]{1,0:T(8,128)S(1)} %get-tuple-element.336, f32[4,512,128]{2,1,0:T(8,128)} %get-tuple-element.335, s32[]{:T(128)} %get-tuple-element.321, pred[512]{0:T(512)(128)(4,1)S(1)} %dynamic-slice_reduce_fusion.5), kind=kOutput, calls=%fused_computation.55.clone.1 | convolution fusion | flops 403439104 | bytes 1575936 | tf_op jit(solution)/shard_map/while/body/eval_jaxpr/dot_general | solution.py:18
  78.3 0.2 fusion.47
  78.6 2.9 %convolution_add_fusion.4 = f32[512,128]{1,0:T(8,128)S(1)} fusion(f32[512,512]{1,0:T(8,128)S(1)} %get-tuple-element.267, f32[512]{0:T(512)S(1)} %max.10, pred[512]{0:T(512)(128)(4,1)S(1)} %dynamic-slice_reduce_fusion.5, f32[4,512,128]{2,1,0:T(8,128)} %get-tuple-element.337, s32[]{:T(128)} %get-tuple-element.321, ...), kind=kOutput, calls=%fused_computation.2.clone.1 | convolution fusion | flops 403308544 | bytes 1840128 | tf_op jit(solution)/shard_map/while/body/eval_jaxpr/dot_general | solution.py:42
  81.5 2.0 %fusion.46 = (f32[512]{0:T(512)S(1)}, f32[512,512]{1,0:T(8,128)S(1)}) fusion(f32[512,128]{1,0:T(8,128)S(1)} %get-tuple-element.336, f32[4,512,128]{2,1,0:T(8,128)} %get-tuple-element.335, s32[]{:T(128)} %get-tuple-element.321, pred[512]{0:T(512)(128)(4,1)S(1)} %dynamic-slice_reduce_fusion.5), kind=kOutput, calls=%fused_computation.55.clone.1 | convolution fusion | flops 403439104 | bytes 1575936 | tf_op jit(solution)/shard_map/while/body/eval_jaxpr/dot_general | solution.py:18
  83.5 0.2 fusion.47
  83.7 2.9 %convolution_add_fusion.4 = f32[512,128]{1,0:T(8,128)S(1)} fusion(f32[512,512]{1,0:T(8,128)S(1)} %get-tuple-element.267, f32[512]{0:T(512)S(1)} %max.10, pred[512]{0:T(512)(128)(4,1)S(1)} %dynamic-slice_reduce_fusion.5, f32[4,512,128]{2,1,0:T(8,128)} %get-tuple-element.337, s32[]{:T(128)} %get-tuple-element.321, ...), kind=kOutput, calls=%fused_computation.2.clone.1 | convolution fusion | flops 403308544 | bytes 1840128 | tf_op jit(solution)/shard_map/while/body/eval_jaxpr/dot_general | solution.py:42
  86.7 2.0 %fusion.46 = (f32[512]{0:T(512)S(1)}, f32[512,512]{1,0:T(8,128)S(1)}) fusion(f32[512,128]{1,0:T(8,128)S(1)} %get-tuple-element.336, f32[4,512,128]{2,1,0:T(8,128)} %get-tuple-element.335, s32[]{:T(128)} %get-tuple-element.321, pred[512]{0:T(512)(128)(4,1)S(1)} %dynamic-slice_reduce_fusion.5), kind=kOutput, calls=%fused_computation.55.clone.1 | convolution fusion | flops 403439104 | bytes 1575936 | tf_op jit(solution)/shard_map/while/body/eval_jaxpr/dot_general | solution.py:18
  88.7 0.2 fusion.47
  88.9 2.9 %convolution_add_fusion.4 = f32[512,128]{1,0:T(8,128)S(1)} fusion(f32[512,512]{1,0:T(8,128)S(1)} %get-tuple-element.267, f32[512]{0:T(512)S(1)} %max.10, pred[512]{0:T(512)(128)(4,1)S(1)} %dynamic-slice_reduce_fusion.5, f32[4,512,128]{2,1,0:T(8,128)} %get-tuple-element.337, s32[]{:T(128)} %get-tuple-element.321, ...), kind=kOutput, calls=%fused_computation.2.clone.1 | convolution fusion | flops 403308544 | bytes 1840128 | tf_op jit(solution)/shard_map/while/body/eval_jaxpr/dot_general | solution.py:42
  91.9 0.8 broadcast_divide_fusion
  (56 shorter events, 0.5 us)
Async XLA Ops:
  6.5 17.5 %copy-start = (s32[4,2,2]{0,2,1:T(2,128)S(1)}, s32[4,2,2]{0,2,1:T(2,128)}, u32[]{:S(2)}) copy-start(s32[4,2,2]{0,2,1:T(2,128)} %param.13) | copy-start | bytes 196
  6.5 13.9 %copy-start.2 = (f32[512,128]{1,0:T(8,128)S(1)}, f32[512,128]{1,0:T(8,128)}, u32[]{:S(2)}) copy-start(f32[512,128]{1,0:T(8,128)} %param.11) | copy-start | bytes 786436
  6.5 64.5 %all-gather.5.cloned.1.call-start = ((), (), s32[]{:S(2)}) async-start(), calls=%async_computation.1 | async-start | bytes 1310720 | tf_op jit(solution)/shard_map/all_gather | solution.py:97
  7.3 63.8 %all-gather.3.cloned.1.call-start = ((), (), s32[]{:S(2)}) async-start(), calls=%async_computation | async-start | bytes 1310720 | tf_op jit(solution)/shard_map/all_gather | solution.py:96
  7.3 20.8 %collective-permute-start = (f32[512,128]{1,0:T(8,128)}, f32[512,128]{1,0:T(8,128)S(1)}, u32[]{:S(2)}, u32[]{:S(2)}) collective-permute-start(f32[512,128]{1,0:T(8,128)} %param.10), channel_id=1, source_target_pairs={{0,4},{4,8},{8,12},{1,5},{5,9},{9,13},{2,6},{6,10},{10,14},{3,7},{... | collective-permute-start | bytes 786440 | tf_op jit(solution)/shard_map/ppermute | solution.py:14
  12.3 17.1 %collective-permute-start.1 = (f32[512,128]{1,0:T(8,128)}, f32[512,128]{1,0:T(8,128)S(1)}, u32[]{:S(2)}, u32[]{:S(2)}) collective-permute-start(f32[512,128]{1,0:T(8,128)} %param.10), channel_id=1, source_target_pairs={{4,0},{8,4},{12,8},{5,1},{9,5},{13,9},{6,2},{10,6},{14,10},{7,3},{... | collective-permute-start | bytes 786440 | tf_op jit(solution)/shard_map/ppermute | solution.py:14
  13.6 22.3 %collective-permute-start.2 = (f32[512,128]{1,0:T(8,128)}, f32[512,128]{1,0:T(8,128)S(1)}, u32[]{:S(2)}, u32[]{:S(2)}) collective-permute-start(f32[512,128]{1,0:T(8,128)} %param.10), channel_id=1, source_target_pairs={{0,8},{4,12},{1,9},{5,13},{2,10},{6,14},{3,11},{7,15},{16,24},{20,... | collective-permute-start | bytes 786440 | tf_op jit(solution)/shard_map/ppermute | solution.py:14
  19.2 18.2 %collective-permute-start.3 = (f32[512,128]{1,0:T(8,128)}, f32[512,128]{1,0:T(8,128)S(1)}, u32[]{:S(2)}, u32[]{:S(2)}) collective-permute-start(f32[512,128]{1,0:T(8,128)} %param.10), channel_id=1, source_target_pairs={{8,0},{12,4},{9,1},{13,5},{10,2},{14,6},{11,3},{15,7},{24,16},{28,... | collective-permute-start | bytes 786440 | tf_op jit(solution)/shard_map/ppermute | solution.py:14
  20.5 17.0 %collective-permute-start.4 = (f32[512,128]{1,0:T(8,128)S(1)}, f32[512,128]{1,0:T(8,128)S(1)}, u32[]{:S(2)}, u32[]{:S(2)}) collective-permute-start(f32[512,128]{1,0:T(8,128)S(1)} %copy-done.2), channel_id=1, source_target_pairs={{0,4},{4,8},{8,12},{1,5},{5,9},{9,13},{2,6},{6,10},{10,14},{3,7},{... | collective-permute-start | bytes 786440 | tf_op jit(solution)/shard_map/ppermute | solution.py:14
  28.1 12.9 %collective-permute-start.5 = (f32[512,128]{1,0:T(8,128)S(1)}, f32[512,128]{1,0:T(8,128)S(1)}, u32[]{:S(2)}, u32[]{:S(2)}) collective-permute-start(f32[512,128]{1,0:T(8,128)S(1)} %copy-done.2), channel_id=1, source_target_pairs={{4,0},{8,4},{12,8},{5,1},{9,5},{13,9},{6,2},{10,6},{14,10},{7,3},{... | collective-permute-start | bytes 786440 | tf_op jit(solution)/shard_map/ppermute | solution.py:14
  29.4 11.6 %collective-permute-start.6 = (f32[512,128]{1,0:T(8,128)S(1)}, f32[512,128]{1,0:T(8,128)S(1)}, u32[]{:S(2)}, u32[]{:S(2)}) collective-permute-start(f32[512,128]{1,0:T(8,128)S(1)} %copy-done.2), channel_id=1, source_target_pairs={{0,8},{4,12},{1,9},{5,13},{2,10},{6,14},{3,11},{7,15},{16,24},{20,... | collective-permute-start | bytes 786440 | tf_op jit(solution)/shard_map/ppermute | solution.py:14
  35.9 16.1 %collective-permute-start.7 = (f32[512,128]{1,0:T(8,128)S(1)}, f32[512,128]{1,0:T(8,128)}, u32[]{:S(2)}, u32[]{:S(2)}) collective-permute-start(f32[512,128]{1,0:T(8,128)S(1)} %copy-done.2), channel_id=1, source_target_pairs={{8,0},{12,4},{9,1},{13,5},{10,2},{14,6},{11,3},{15,7},{24,16},{28,... | collective-permute-start | bytes 786440 | tf_op jit(solution)/shard_map/ppermute | solution.py:14
  37.4 16.6 %copy-start.1 = (f32[512,128]{1,0:T(8,128)S(1)}, f32[512,128]{1,0:T(8,128)}, u32[]{:S(2)}) copy-start(f32[512,128]{1,0:T(8,128)} %param.9) | copy-start | bytes 786436
Sparse Core Ops, SparseCore 0:
  8.9 19.4 all-gather.4
  29.9 16.6 all-gather.2
where the time goes:
time: 100 us; the launch traced here: 99.6 us
  matrix products  35.4 us (35%)
  starting transfers between devices  25.8 us (26%)
  between operations  16 us (16%)
  waiting for transfers between devices  15.3 us (15%)
  other arithmetic  5.6 us (6%)
  local copies, waits for them, and re-layouts  1.14 us (1%)
    ppermute x8, starting transfers between devices, shifted(): return lax.ppermute(block, axis, route)  25.7 us
    dot_general x8, matrix products, absorb_block(): jnp.dot(weights, value_block, precision=lax.Precision.HIGHEST, preferred_...  23.2 us
    ppermute x8, waiting for transfers between devices, shifted(): return lax.ppermute(block, axis, route)  14.5 us
    dot_general x8, matrix products, score_block(): lax.dot_general(query_rows, key_rows, (((1,), (1,)), ((), ())), precision...  12.2 us
    concatenate x1, other arithmetic, per_device(): jnp.concatenate(far_values, axis=0)  2.02 us
  transfers between devices with their start and end apart: 10, of which 2 were waited for; matrix products, arithmetic and copies ran while one was open for 21% of the time, Pallas kernels for 0%

commit v1 on v0

v1 whole, which is shorter than its diff:
```python
import functools
import math

import jax
import jax.numpy as jnp
from jax import lax
from jax.experimental import pallas as pl
from jax.experimental.pallas import tpu as pltpu
from jax.sharding import PartitionSpec as P


masked_score = -1e30
lane_count = 128
row_chunk = 256
call_blocks = 4
kernel_vmem = 24 * 2**20


def halves(x):
    high = x.astype(jnp.bfloat16)
    return high, (x - high.astype(jnp.float32)).astype(jnp.bfloat16)


def fold_lanes(x, op):
    folded = x[:, :lane_count]
    for start in range(lane_count, x.shape[1], lane_count):
        folded = op(folded, x[:, start : start + lane_count])
    return folded


def absorb(state, query_parts, key_parts, value_parts, enabled):
    scores = lax.dot_general(
        query_parts, key_parts, (((1,), (1,)), ((), ())), preferred_element_type=jnp.float32
    )
    block_max = jnp.max(fold_lanes(scores, jnp.maximum), axis=1, keepdims=True)
    if enabled is not None:
        block_max = jnp.where(enabled, block_max, masked_score)
    new_max = block_max if state is None else jnp.maximum(state[0], block_max)
    shift = new_max if enabled is None else jnp.where(enabled, new_max, -masked_score)
    weights = jnp.exp2(scores - shift)
    total = fold_lanes(weights, jnp.add)
    weights_high, weights_low = halves(weights)
    weighted = jnp.dot(weights_high, value_parts, preferred_element_type=jnp.float32)
    weighted += jnp.dot(weights_low, value_parts, preferred_element_type=jnp.float32)
    if state is None:
        return new_max, total, weighted
    factor = jnp.exp2(state[0] - new_max)
    return new_max, state[1] * factor + total, state[2] * factor + weighted


def partner_of(index, distance, parity):
    return jnp.where((index // distance) % 2 == parity, index + distance, index - distance)


def block_flag(which, block_mask, partner_flags):
    axis, distance, parity = which
    if axis == "space":
        index = lax.axis_index("space")
        partner = partner_of(index, distance, parity)
        inside = (partner >= 0) & (partner < block_mask.shape[1])
        return inside & (block_mask[index, jnp.clip(partner, 0, block_mask.shape[1] - 1)] > 0)
    index = lax.axis_index("frame")
    if axis == "relay":
        partner = jnp.where(index % 2 == parity, index + distance, index - distance)
    else:
        partner = partner_of(index, distance, parity)
    inside = (partner >= 0) & (partner < partner_flags.shape[0])
    upper = jnp.where(partner > index, 1, 0)
    return inside & (partner_flags[index, distance.bit_length() - 1, upper] > 0)


def attend_kernel(plan, first, last, block_mask, partner_flags, queries, *refs):
    position = 0
    key_parts = []
    value_parts = []
    enabled = []
    for kind, which in plan:
        if kind == "stacked":
            rows = refs[position].shape[0] // 2
            key_rows, value_rows = refs[position][:rows, :], refs[position][rows:, :]
            position += 1
        else:
            key_rows, value_rows = refs[position][...], refs[position + 1][...]
            position += 2
        flag = None if which is None else block_flag(which[0], block_mask, partner_flags)
        if kind == "either":
            other = block_flag(which[1], block_mask, partner_flags)
            key_rows = jnp.where(flag, key_rows, refs[position][...])
            value_rows = jnp.where(flag, value_rows, refs[position + 1][...])
            position += 2
            flag = flag | other
        key_high, key_low = halves(key_rows)
        key_parts.append(jnp.concatenate([key_high, key_high, key_low, key_low], axis=1))
        value_parts.append(jnp.concatenate(halves(value_rows), axis=1))
        enabled.append(flag)
    carried = () if first else refs[position : position + 3]
    outs = refs[position + len(carried) :]
    row_count, width = queries.shape
    chunk = min(row_chunk, row_count)
    score_scale = math.log2(math.e) / math.sqrt(width)
    for start in range(0, row_count, chunk):
        rows = slice(start, start + chunk)
        query_high, query_low = halves(queries[rows, :] * score_scale)
        query_parts = jnp.concatenate([query_high, query_low, query_high, query_low], axis=1)
        state = None if first else (carried[0][rows, :1], carried[1][rows, :], carried[2][rows, :])
        for index in range(len(plan)):
            state = absorb(state, query_parts, key_parts[index], value_parts[index], enabled[index])
        running_max, total, weighted = state
        if last:
            row_total = jnp.sum(total, axis=1, keepdims=True)
            outs[0][rows, :] = (weighted[:, :width] + weighted[:, width:]) / row_total
        else:
            outs[0][rows, :] = jnp.broadcast_to(running_max, (chunk, lane_count))
            outs[1][rows, :] = total
            outs[2][rows, :] = weighted


def attend(state, tables, queries, blocks, last=False):
    row_count, width = queries.shape
    plan = tuple((kind, which) for kind, which, _ in blocks)
    arrays = [array for _, _, group in blocks for array in group]
    first = state is None
    operands = [*tables, queries, *arrays, *(() if first else state)]
    whole = pl.BlockSpec(memory_space=pltpu.VMEM)
    if last:
        out_shape = jax.ShapeDtypeStruct((row_count, width), jnp.float32)
    else:
        out_shape = (
            jax.ShapeDtypeStruct((row_count, lane_count), jnp.float32),
            jax.ShapeDtypeStruct((row_count, lane_count), jnp.float32),
            jax.ShapeDtypeStruct((row_count, 2 * width), jnp.float32),
        )
    work = len(blocks) * row_count * row_count
    return pl.pallas_call(
        functools.partial(attend_kernel, plan, first, last),
        in_specs=[pl.BlockSpec(memory_space=pltpu.SMEM)] * 2 + [whole] * (len(operands) - 2),
        out_specs=whole if last else (whole,) * 3,
        out_shape=out_shape,
        compiler_params=pltpu.CompilerParams(vmem_limit_bytes=kernel_vmem),
        cost_estimate=pl.CostEstimate(
            flops=16 * work * width, bytes_accessed=8 * len(blocks) * row_count * width, transcendentals=work
        ),
    )(*operands)


def attend_all(state, tables, queries, blocks, last=False):
    for start in range(0, len(blocks), call_blocks):
        part = blocks[start : start + call_blocks]
        state = attend(state, tables, queries, part, last and start + call_blocks >= len(blocks))
    return state


def matching(size, distance, parity):
    lower = [i for i in range(size - distance) if (i // distance) % 2 == parity]
    return [(i, i + distance) for i in lower] + [(i + distance, i) for i in lower]


def attention(queries, keys, values, block_mask, partner_flags):
    blocks = lax.axis_size("space")
    groups = lax.axis_size("frame")
    levels = partner_flags.shape[1]
    tables = (block_mask, partner_flags)

    near = {}
    for parity in (1, 0):
        route = matching(groups, 1, parity)
        if route:
            near[parity] = (lax.ppermute(keys, "frame", route), lax.ppermute(values, "frame", route))
    near_blocks = [("pair", (("frame", 1, parity),), arrays) for parity, arrays in near.items()]

    far = {}
    if levels > 1:
        for parity in (1, 0):
            other = 1 - parity
            if other not in near:
                continue
            holders = {target for _, target in matching(groups, 1, other)}
            route = [pair for pair in matching(groups, 1, parity) if pair[0] in holders]
            if route:
                far[parity] = (
                    lax.ppermute(near[other][0], "frame", route), lax.ppermute(near[other][1], "frame", route)
                )
    far_blocks = [("pair", (("relay", 2, parity),), arrays) for parity, arrays in far.items()]
    if len(far_blocks) == 2 and groups <= 4:
        (_, (one,), here), (_, (two,), there) = far_blocks
        far_blocks = [("either", (one, two), (*here, *there))]
    for level in range(2, levels):
        for parity in (0, 1):
            route = matching(groups, 2**level, parity)
            if route:
                arrays = tuple(lax.ppermute(array, "frame", route) for array in (keys, values))
                far_blocks.append(("pair", (("frame", 2**level, parity),), arrays))

    window_blocks = []
    half = blocks // 2
    if half:
        route = matching(blocks, half, 0)
        arrays = (lax.ppermute(keys, "space", route), lax.ppermute(values, "space", route))
        window_blocks.append(("pair", (("space", half, 0),), arrays))
    side_blocks = []
    stacked = jnp.concatenate([keys, values], axis=0)
    for distance in range(half - 1, 0, -1):
        for parity in (0, 1):
            route = matching(blocks, distance, parity)
            if route:
                array = lax.ppermute(stacked, "space", route)
                side_blocks.append(("stacked", (("space", distance, parity),), (array,)))

    state = attend(None, tables, queries, [("pair", None, (keys, values))])
    state = attend_all(state, tables, queries, near_blocks + window_blocks + side_blocks[:1])
    state = attend_all(state, tables, queries, side_blocks[1:])
    return attend_all(state, tables, queries, far_blocks, last=True)


def solution(mesh):
    rows = P(("groups", "frame", "space"), None)
    return jax.shard_map(attention, mesh=mesh, in_specs=(rows, rows, rows, P(), P()), out_specs=rows, check_vma=False)
```

time: 100 us -> 50.4 us (0.50)
  matrix products: 35.4 us -> 0 us
  between operations: 16 us -> 0.15 us
  Pallas kernels: 0 us -> 10.3 us
  starting transfers between devices: 25.8 us -> 15.6 us
  waiting for transfers between devices: 15.3 us -> 21.6 us
  other arithmetic: 5.6 us -> 0 us
  local copies, waits for them, and re-layouts: 1.14 us -> 2.49 us
    dot_general x16 -> x0, matrix products: 35.4 us -> none  [the longest x8 23.2 us: absorb_block(): jnp.dot(weights, value_block, precision=lax.Precision.HIGHEST, preferred_...]
    pallas_call x0 -> x4, Pallas kernels: none -> 10.3 us  [attend(): pl.pallas_call(functools.partial(attend_kernel, plan, first, last), in_sp...]
    ppermute x8 -> x12, starting transfers between devices: 25.7 us -> 15.6 us  [the longest x2 5.13 us: attention(): lax.ppermute(values, 'frame', route)]
    ppermute x8 -> x12, waiting for transfers between devices: 14.5 us -> 21.6 us  [the longest x1 12.4 us: attention(): lax.ppermute(values, 'space', route)]
    concatenate x3 -> x0, other arithmetic: 2.1 us -> none  [the longest x1 2.02 us: per_device(): jnp.concatenate(far_values, axis=0)]
    unnamed x6 -> x12, local copies, waits for them, and re-layouts: 0.01 us -> 1.79 us
    reduce_sum x8 -> x0, other arithmetic: 1.69 us -> none  [absorb_block(): row_total = row_total * factor + jnp.sum(weights, axis=1)]
  transfers between devices with their start and end apart: 10 -> 12, of which waited for: 2 -> 5; matrix products, arithmetic and copies ran while one was open for 21% -> 5% of each run, Pallas kernels for 0% -> 15%
where the time goes in v1:
time: 50.4 us; the launch traced here: 50.2 us
  waiting for transfers between devices  21.6 us (43%)
  starting transfers between devices  15.6 us (31%)
  Pallas kernels  10.3 us (20%)
  local copies, waits for them, and re-layouts  2.49 us (5%)
    ppermute x1, waiting for transfers between devices, attention(): lax.ppermute(values, 'space', route)  12.4 us
    pallas_call x4, Pallas kernels, attend(): pl.pallas_call(functools.partial(attend_kernel, plan, first, last), in_sp...  10.3 us
    ppermute x2, starting transfers between devices, attention(): lax.ppermute(values, 'frame', route)  5.13 us
    ppermute x2, starting transfers between devices, attention(): lax.ppermute(keys, 'frame', route)  3.72 us
    ppermute x2, waiting for transfers between devices, attention(): lax.ppermute(near[other][1], 'frame', route)  3.22 us
    ppermute x2, waiting for transfers between devices, attention(): lax.ppermute(values, 'frame', route)  3.1 us
    ppermute x1, waiting for transfers between devices, attention(): lax.ppermute(keys, 'space', route)  2.13 us
    ppermute x2, starting transfers between devices, attention(): lax.ppermute(near[other][1], 'frame', route)  1.96 us
  transfers between devices with their start and end apart: 12, of which 5 were waited for; matrix products, arithmetic and copies ran while one was open for 5% of the time, Pallas kernels for 15%

profile of v1, /device:TPU:0, one launch (start us, length us, event | category | flops | bytes accessed | tf_op | source)
XLA Modules:
  0.0 50.2 jit_solution(3796941722206998334)
XLA Ops:
  0.0 0.0 copy-start.2
  0.0 3.1 %collective-permute-start = (f32[512,128]{1,0:T(8,128)}, f32[512,128]{1,0:T(8,128)S(1)}, u32[]{:S(2)}, u32[]{:S(2)}) collective-permute-start(f32[512,128]{1,0:T(8,128)} %refs_0_.1), channel_id=1, source_target_pairs={{0,4},{8,12},{4,0},{12,8},{1,5},{9,13},{5,1},{13,9},{2,6},{10,14},... | collective-permute-start | bytes 786440 | tf_op jit(solution)/shard_map/ppermute | solution.py:168
  3.1 0.7 %collective-permute-start.4 = (f32[512,128]{1,0:T(8,128)}, f32[512,128]{1,0:T(8,128)S(1)}, u32[]{:S(2)}, u32[]{:S(2)}) collective-permute-start(f32[512,128]{1,0:T(8,128)} %refs_0_.1), channel_id=1, source_target_pairs={{4,8},{8,4},{5,9},{9,5},{6,10},{10,6},{7,11},{11,7},{20,24},{24,20... | collective-permute-start | bytes 786440 | tf_op jit(solution)/shard_map/ppermute | solution.py:168
  3.7 4.5 %collective-permute-start.2 = (f32[512,128]{1,0:T(8,128)}, f32[512,128]{1,0:T(8,128)S(1)}, u32[]{:S(2)}, u32[]{:S(2)}) collective-permute-start(f32[512,128]{1,0:T(8,128)} %refs_1_.1), channel_id=1, source_target_pairs={{0,4},{8,12},{4,0},{12,8},{1,5},{9,13},{5,1},{13,9},{2,6},{10,14},... | collective-permute-start | bytes 786440 | tf_op jit(solution)/shard_map/ppermute | solution.py:168
  8.2 0.0 copy-start.4
  8.2 1.7 %constant_dynamic-update-slice_fusion.1 = f32[1024,128]{1,0:T(8,128)} fusion(f32[512,128]{1,0:T(8,128)} %refs_0_.1), kind=kLoop, calls=%fused_computation.1 | loop fusion | bytes 524288
  9.9 0.0 copy-done.2
  9.9 0.0 copy-start.1
  9.9 0.0 copy-start
  9.9 0.7 %constant_dynamic-update-slice_fusion = f32[1024,128]{1,0:T(8,128)} fusion(f32[1024,128]{1,0:T(8,128)} %constant_dynamic-update-slice_fusion.1, f32[512,128]{1,0:T(8,128)S(1)} %copy-done.2), kind=kLoop, calls=%fused_computation | loop fusion | bytes 524288 | tf_op jit(solution)/shard_map/concatenate | solution.py:201
  10.6 0.0 copy-start.3
  10.6 0.0 collective-permute-start.11
  10.6 0.8 %collective-permute-start.8 = (f32[1024,128]{1,0:T(8,128)}, f32[1024,128]{1,0:T(8,128)S(1)}, u32[]{:S(2)}, u32[]{:S(2)}) collective-permute-start(f32[1024,128]{1,0:T(8,128)} %constant_dynamic-update-slice_fusion), channel_id=1, source_target_pairs={{1,2},{2,1},{5,6},{6,5},{9,10},{10,9},{13,14},{14,13},{17,18},{18,... | collective-permute-start | bytes 1572872 | tf_op jit(solution)/shard_map/ppermute | solution.py:206
  11.4 0.0 collective-permute-done.refs_2_
  11.4 0.7 %collective-permute-start.6 = (f32[512,128]{1,0:T(8,128)S(1)}, f32[512,128]{1,0:T(8,128)S(1)}, u32[]{:S(2)}, u32[]{:S(2)}) collective-permute-start(f32[512,128]{1,0:T(8,128)S(1)} %copy-done.2), channel_id=1, source_target_pairs={{4,8},{8,4},{5,9},{9,5},{6,10},{10,6},{7,11},{11,7},{20,24},{24,20... | collective-permute-start | bytes 786440 | tf_op jit(solution)/shard_map/ppermute | solution.py:168
  12.1 3.1 %collective-permute-done.2.refs_3_ = f32[512,128]{1,0:T(8,128)S(1)} collective-permute-done((f32[512,128]{1,0:T(8,128)}, f32[512,128]{1,0:T(8,128)S(1)}, u32[]{:S(2)}, u32[]{:S(2)}) %collective-permute-start.2) | collective-permute-done | bytes 262176 | tf_op jit(solution)/shard_map/ppermute | solution.py:168
  15.2 1.7 %collective-permute-start.10 = (f32[512,128]{1,0:T(8,128)S(1)}, f32[512,128]{1,0:T(8,128)S(1)}, u32[]{:S(2)}, u32[]{:S(2)}) collective-permute-start(f32[512,128]{1,0:T(8,128)S(1)} %copy-done.2), channel_id=1, source_target_pairs={{0,2},{1,3},{2,0},{3,1},{4,6},{5,7},{6,4},{7,5},{8,10},{9,11},{10,... | collective-permute-start | bytes 786440 | tf_op jit(solution)/shard_map/ppermute | solution.py:198
  16.8 0.0 collective-permute-done.4.refs_0_
  16.8 0.0 copy-done.1
  16.9 0.4 collective-permute-start.9
  17.2 0.0 copy-done.4
  17.2 0.1 copy.9.partner_flags
  17.3 0.0 collective-permute-done.6.refs_1_
  17.3 0.7 %collective-permute-start.1 = (f32[512,128]{1,0:T(8,128)S(1)}, f32[512,128]{1,0:T(8,128)S(1)}, u32[]{:S(2)}, u32[]{:S(2)}) collective-permute-start(f32[512,128]{1,0:T(8,128)S(1)} %collective-permute-done.refs_2_), channel_id=1, source_target_pairs={{4,8},{8,4},{5,9},{9,5},{6,10},{10,6},{7,11},{11,7},{20,24},{24,20... | collective-permute-start | bytes 786440 | tf_op jit(solution)/shard_map/ppermute | solution.py:181
  18.0 12.4 %collective-permute-done.10.refs_5_ = f32[512,128]{1,0:T(8,128)S(1)} collective-permute-done((f32[512,128]{1,0:T(8,128)S(1)}, f32[512,128]{1,0:T(8,128)S(1)}, u32[]{:S(2)}, u32[]{:S(2)}) %collective-permute-start.10) | collective-permute-done | bytes 262176 | tf_op jit(solution)/shard_map/ppermute | solution.py:198
  30.4 0.7 %collective-permute-start.3 = (f32[512,128]{1,0:T(8,128)S(1)}, f32[512,128]{1,0:T(8,128)S(1)}, u32[]{:S(2)}, u32[]{:S(2)}) collective-permute-start(f32[512,128]{1,0:T(8,128)S(1)} %collective-permute-done.2.refs_3_), channel_id=1, source_target_pairs={{4,8},{8,4},{5,9},{9,5},{6,10},{10,6},{7,11},{11,7},{20,24},{24,20... | collective-permute-start | bytes 786440 | tf_op jit(solution)/shard_map/ppermute | solution.py:181
  31.1 2.1 %collective-permute-done.9.refs_4_ = f32[512,128]{1,0:T(8,128)S(1)} collective-permute-done((f32[512,128]{1,0:T(8,128)S(1)}, f32[512,128]{1,0:T(8,128)S(1)}, u32[]{:S(2)}, u32[]{:S(2)}) %collective-permute-start.9) | collective-permute-done | bytes 262176 | tf_op jit(solution)/shard_map/ppermute | solution.py:198
  33.2 1.3 %collective-permute-start.5 = (f32[512,128]{1,0:T(8,128)S(1)}, f32[512,128]{1,0:T(8,128)S(1)}, u32[]{:S(2)}, u32[]{:S(2)}) collective-permute-start(f32[512,128]{1,0:T(8,128)S(1)} %collective-permute-done.4.refs_0_), channel_id=1, source_target_pairs={{8,12},{4,0},{9,13},{5,1},{10,14},{6,2},{11,15},{7,3},{24,28},{20,... | collective-permute-start | bytes 786440 | tf_op jit(solution)/shard_map/ppermute | solution.py:181
  34.5 0.0 collective-permute-done.11.refs_6_
  34.5 1.3 %collective-permute-start.7 = (f32[512,128]{1,0:T(8,128)S(1)}, f32[512,128]{1,0:T(8,128)S(1)}, u32[]{:S(2)}, u32[]{:S(2)}) collective-permute-start(f32[512,128]{1,0:T(8,128)S(1)} %collective-permute-done.6.refs_1_), channel_id=1, source_target_pairs={{8,12},{4,0},{9,13},{5,1},{10,14},{6,2},{11,15},{7,3},{24,28},{20,... | collective-permute-start | bytes 786440 | tf_op jit(solution)/shard_map/ppermute | solution.py:181
  35.8 0.0 copy-done
  35.8 0.0 copy-done.3
  35.8 1.8 %shard_map.55 = (f32[512,128]{1,0:T(8,128)S(1)}, f32[512,128]{1,0:T(8,128)S(1)}, f32[512,256]{1,0:T(8,128)S(1)}) custom-call(s32[4,4]{1,0:T(4,128)S(1)} %copy-done.3, s32[4,2,2]{2,1,0:T(2,128)S(1)} %copy.9.partner_flags, f32[512,128]{1,0:T(8,128)S(1)} %copy-done, f32[512,128]{1,0:T(8,128)S(1)} %copy-done.1, f32[512,128]{1,0:T(8,128)S(1)} %copy-done.2), custom_call_target="tpu_custom_call" | custom-call | flops 536870912 | bytes 524288 | tf_op jit(solution)/shard_map/pallas_call | solution.py:134
  37.6 3.9 %shard_map.56 = (f32[512,128]{1,0:T(8,128)S(1)}, f32[512,128]{1,0:T(8,128)S(1)}, f32[512,256]{1,0:T(8,128)S(1)}) custom-call(s32[4,4]{1,0:T(4,128)S(1)} %copy-done.3, s32[4,2,2]{2,1,0:T(2,128)S(1)} %copy.9.partner_flags, f32[512,128]{1,0:T(8,128)S(1)} %copy-done, f32[512,128]{1,0:T(8,128)S(1)} %collective-permute-done.4.refs_0_, ...), custom_call_target="tpu_custom_call" | custom-call | flops 2147483648 | bytes 2097152 | tf_op jit(solution)/shard_map/pallas_call | solution.py:134
  41.5 0.0 collective-permute-done.8.refs_0_
  41.5 2.0 %shard_map.57 = (f32[512,128]{1,0:T(8,128)S(1)}, f32[512,128]{1,0:T(8,128)S(1)}, f32[512,256]{1,0:T(8,128)S(1)}) custom-call(s32[4,4]{1,0:T(4,128)S(1)} %copy-done.3, s32[4,2,2]{2,1,0:T(2,128)S(1)} %copy.9.partner_flags, f32[512,128]{1,0:T(8,128)S(1)} %copy-done, f32[1024,128]{1,0:T(8,128)S(1)} %collective-permute-done.8.refs_0_, ...), custom_call_target="tpu_custom_call" | custom-call | flops 536870912 | bytes 524288 | tf_op jit(solution)/shard_map/pallas_call | solution.py:134
  43.5 0.0 collective-permute-done.1.refs_0_
  43.5 0.0 collective-permute-done.3.refs_1_
  43.5 0.7 %collective-permute-done.5.refs_2_ = f32[512,128]{1,0:T(8,128)S(1)} collective-permute-done((f32[512,128]{1,0:T(8,128)S(1)}, f32[512,128]{1,0:T(8,128)S(1)}, u32[]{:S(2)}, u32[]{:S(2)}) %collective-permute-start.5) | collective-permute-done | bytes 262176 | tf_op jit(solution)/shard_map/ppermute | solution.py:181
  44.3 3.2 %collective-permute-done.7.refs_3_ = f32[512,128]{1,0:T(8,128)S(1)} collective-permute-done((f32[512,128]{1,0:T(8,128)S(1)}, f32[512,128]{1,0:T(8,128)S(1)}, u32[]{:S(2)}, u32[]{:S(2)}) %collective-permute-start.7) | collective-permute-done | bytes 262176 | tf_op jit(solution)/shard_map/ppermute | solution.py:181
  47.5 2.7 %shard_map.58 = f32[512,128]{1,0:T(8,128)} custom-call(s32[4,4]{1,0:T(4,128)S(1)} %copy-done.3, s32[4,2,2]{2,1,0:T(2,128)S(1)} %copy.9.partner_flags, f32[512,128]{1,0:T(8,128)S(1)} %copy-done, f32[512,128]{1,0:T(8,128)S(1)} %collective-permute-done.1.refs_0_, f32[512,128]{1,0:T(8,128)S(1)} %collective-permute-done.3.refs_1_, ...), custom_call_target="tpu_custom_call" | custom-call | flops 536870912 | bytes 524288 | tf_op jit(solution)/shard_map/pallas_call | solution.py:134
Async XLA Ops:
  0.0 9.9 %copy-start.2 = (f32[512,128]{1,0:T(8,128)S(1)}, f32[512,128]{1,0:T(8,128)}, u32[]{:S(2)}) copy-start(f32[512,128]{1,0:T(8,128)} %refs_1_.1) | copy-start | bytes 786436
  0.0 11.4 %collective-permute-start = (f32[512,128]{1,0:T(8,128)}, f32[512,128]{1,0:T(8,128)S(1)}, u32[]{:S(2)}, u32[]{:S(2)}) collective-permute-start(f32[512,128]{1,0:T(8,128)} %refs_0_.1), channel_id=1, source_target_pairs={{0,4},{8,12},{4,0},{12,8},{1,5},{9,13},{5,1},{13,9},{2,6},{10,14},... | collective-permute-start | bytes 786440 | tf_op jit(solution)/shard_map/ppermute | solution.py:168
  3.1 13.8 %collective-permute-start.4 = (f32[512,128]{1,0:T(8,128)}, f32[512,128]{1,0:T(8,128)S(1)}, u32[]{:S(2)}, u32[]{:S(2)}) collective-permute-start(f32[512,128]{1,0:T(8,128)} %refs_0_.1), channel_id=1, source_target_pairs={{4,8},{8,4},{5,9},{9,5},{6,10},{10,6},{7,11},{11,7},{20,24},{24,20... | collective-permute-start | bytes 786440 | tf_op jit(solution)/shard_map/ppermute | solution.py:168
  3.7 11.5 %collective-permute-start.2 = (f32[512,128]{1,0:T(8,128)}, f32[512,128]{1,0:T(8,128)S(1)}, u32[]{:S(2)}, u32[]{:S(2)}) collective-permute-start(f32[512,128]{1,0:T(8,128)} %refs_1_.1), channel_id=1, source_target_pairs={{0,4},{8,12},{4,0},{12,8},{1,5},{9,13},{5,1},{13,9},{2,6},{10,14},... | collective-permute-start | bytes 786440 | tf_op jit(solution)/shard_map/ppermute | solution.py:168
  8.2 9.0 %copy-start.4 = (s32[4,2,2]{0,2,1:T(2,128)S(1)}, s32[4,2,2]{0,2,1:T(2,128)}, u32[]{:S(2)}) copy-start(s32[4,2,2]{0,2,1:T(2,128)} %param.9) | copy-start | bytes 196
  9.9 7.0 %copy-start.1 = (f32[512,128]{1,0:T(8,128)S(1)}, f32[512,128]{1,0:T(8,128)}, u32[]{:S(2)}) copy-start(f32[512,128]{1,0:T(8,128)} %refs_0_.1) | copy-start | bytes 786436
  9.9 25.9 %copy-start = (f32[512,128]{1,0:T(8,128)S(1)}, f32[512,128]{1,0:T(8,128)}, u32[]{:S(2)}) copy-start(f32[512,128]{1,0:T(8,128)} %queries.7) | copy-start | bytes 786436
  10.6 25.2 %copy-start.3 = (s32[4,4]{1,0:T(4,128)S(1)}, s32[4,4]{1,0:T(4,128)}, u32[]{:S(2)}) copy-start(s32[4,4]{1,0:T(4,128)} %block_mask.7) | copy-start | bytes 196
  10.6 23.9 %collective-permute-start.11 = (f32[1024,128]{1,0:T(8,128)}, f32[1024,128]{1,0:T(8,128)S(1)}, u32[]{:S(2)}, u32[]{:S(2)}) collective-permute-start(f32[1024,128]{1,0:T(8,128)} %constant_dynamic-update-slice_fusion), channel_id=1, source_target_pairs={{0,1},{2,3},{1,0},{3,2},{4,5},{6,7},{5,4},{7,6},{8,9},{10,11},{9,8... | collective-permute-start | bytes 1572872 | tf_op jit(solution)/shard_map/ppermute | solution.py:206
  10.6 30.9 %collective-permute-start.8 = (f32[1024,128]{1,0:T(8,128)}, f32[1024,128]{1,0:T(8,128)S(1)}, u32[]{:S(2)}, u32[]{:S(2)}) collective-permute-start(f32[1024,128]{1,0:T(8,128)} %constant_dynamic-update-slice_fusion), channel_id=1, source_target_pairs={{1,2},{2,1},{5,6},{6,5},{9,10},{10,9},{13,14},{14,13},{17,18},{18,... | collective-permute-start | bytes 1572872 | tf_op jit(solution)/shard_map/ppermute | solution.py:206
  11.4 5.9 %collective-permute-start.6 = (f32[512,128]{1,0:T(8,128)S(1)}, f32[512,128]{1,0:T(8,128)S(1)}, u32[]{:S(2)}, u32[]{:S(2)}) collective-permute-start(f32[512,128]{1,0:T(8,128)S(1)} %copy-done.2), channel_id=1, source_target_pairs={{4,8},{8,4},{5,9},{9,5},{6,10},{10,6},{7,11},{11,7},{20,24},{24,20... | collective-permute-start | bytes 786440 | tf_op jit(solution)/shard_map/ppermute | solution.py:168
  15.2 15.2 %collective-permute-start.10 = (f32[512,128]{1,0:T(8,128)S(1)}, f32[512,128]{1,0:T(8,128)S(1)}, u32[]{:S(2)}, u32[]{:S(2)}) collective-permute-start(f32[512,128]{1,0:T(8,128)S(1)} %copy-done.2), channel_id=1, source_target_pairs={{0,2},{1,3},{2,0},{3,1},{4,6},{5,7},{6,4},{7,5},{8,10},{9,11},{10,... | collective-permute-start | bytes 786440 | tf_op jit(solution)/shard_map/ppermute | solution.py:198
  16.9 16.3 %collective-permute-start.9 = (f32[512,128]{1,0:T(8,128)S(1)}, f32[512,128]{1,0:T(8,128)S(1)}, u32[]{:S(2)}, u32[]{:S(2)}) collective-permute-start(f32[512,128]{1,0:T(8,128)S(1)} %copy-done.1), channel_id=1, source_target_pairs={{0,2},{1,3},{2,0},{3,1},{4,6},{5,7},{6,4},{7,5},{8,10},{9,11},{10,... | collective-permute-start | bytes 786440 | tf_op jit(solution)/shard_map/ppermute | solution.py:198
  17.3 26.2 %collective-permute-start.1 = (f32[512,128]{1,0:T(8,128)S(1)}, f32[512,128]{1,0:T(8,128)S(1)}, u32[]{:S(2)}, u32[]{:S(2)}) collective-permute-start(f32[512,128]{1,0:T(8,128)S(1)} %collective-permute-done.refs_2_), channel_id=1, source_target_pairs={{4,8},{8,4},{5,9},{9,5},{6,10},{10,6},{7,11},{11,7},{20,24},{24,20... | collective-permute-start | bytes 786440 | tf_op jit(solution)/shard_map/ppermute | solution.py:181
  30.4 13.1 %collective-permute-start.3 = (f32[512,128]{1,0:T(8,128)S(1)}, f32[512,128]{1,0:T(8,128)S(1)}, u32[]{:S(2)}, u32[]{:S(2)}) collective-permute-start(f32[512,128]{1,0:T(8,128)S(1)} %collective-permute-done.2.refs_3_), channel_id=1, source_target_pairs={{4,8},{8,4},{5,9},{9,5},{6,10},{10,6},{7,11},{11,7},{20,24},{24,20... | collective-permute-start | bytes 786440 | tf_op jit(solution)/shard_map/ppermute | solution.py:181
  33.2 11.1 %collective-permute-start.5 = (f32[512,128]{1,0:T(8,128)S(1)}, f32[512,128]{1,0:T(8,128)S(1)}, u32[]{:S(2)}, u32[]{:S(2)}) collective-permute-start(f32[512,128]{1,0:T(8,128)S(1)} %collective-permute-done.4.refs_0_), channel_id=1, source_target_pairs={{8,12},{4,0},{9,13},{5,1},{10,14},{6,2},{11,15},{7,3},{24,28},{20,... | collective-permute-start | bytes 786440 | tf_op jit(solution)/shard_map/ppermute | solution.py:181
  34.5 13.0 %collective-permute-start.7 = (f32[512,128]{1,0:T(8,128)S(1)}, f32[512,128]{1,0:T(8,128)S(1)}, u32[]{:S(2)}, u32[]{:S(2)}) collective-permute-start(f32[512,128]{1,0:T(8,128)S(1)} %collective-permute-done.6.refs_1_), channel_id=1, source_target_pairs={{8,12},{4,0},{9,13},{5,1},{10,14},{6,2},{11,15},{7,3},{24,28},{20,... | collective-permute-start | bytes 786440 | tf_op jit(solution)/shard_map/ppermute | solution.py:181

commit v2 on v1

v2 whole, which is shorter than its diff:
```python
import functools
import math

import jax
import jax.numpy as jnp
from jax import lax
from jax.experimental import pallas as pl
from jax.experimental.pallas import tpu as pltpu
from jax.sharding import PartitionSpec as P


masked_score = -1e30
lane_count = 128
row_chunk = 256
call_blocks = 4
kernel_vmem = 24 * 2**20
fetch_pieces = 4
far_distance = 2


def halves(x):
    high = x.astype(jnp.bfloat16)
    return high, (x - high.astype(jnp.float32)).astype(jnp.bfloat16)


def fold_lanes(x, op):
    folded = x[:, :lane_count]
    for start in range(lane_count, x.shape[1], lane_count):
        folded = op(folded, x[:, start : start + lane_count])
    return folded


def absorb(state, query_parts, key_parts, value_parts, enabled):
    scores = lax.dot_general(
        query_parts, key_parts, (((1,), (1,)), ((), ())), preferred_element_type=jnp.float32
    )
    block_max = jnp.max(fold_lanes(scores, jnp.maximum), axis=1, keepdims=True)
    if enabled is not None:
        block_max = chosen(enabled, block_max, jnp.full_like(block_max, masked_score))
    new_max = block_max if state is None else jnp.maximum(state[0], block_max)
    shift = new_max if enabled is None else chosen(enabled, new_max, jnp.full_like(new_max, -masked_score))
    weights = jnp.exp2(scores - shift)
    total = fold_lanes(weights, jnp.add)
    weights_high, weights_low = halves(weights)
    weighted = jnp.dot(weights_high, value_parts, preferred_element_type=jnp.float32)
    weighted += jnp.dot(weights_low, value_parts, preferred_element_type=jnp.float32)
    if state is None:
        return new_max, total, weighted
    factor = jnp.exp2(state[0] - new_max)
    return new_max, state[1] * factor + total, state[2] * factor + weighted


def partner_of(index, distance, parity):
    return jnp.where((index // distance) % 2 == parity, index + distance, index - distance)


def entry_of(entries, column):
    columns = lax.broadcasted_iota(jnp.int32, entries.shape, 1)
    return jnp.sum(jnp.where(columns == column, entries, 0).astype(jnp.float32), axis=1, keepdims=True)


def block_flag(which, block_mask, partner_flags):
    axis, distance, parity = which
    if axis == "space":
        index = lax.axis_index("space")
        return entry_of(block_mask[pl.ds(index, 1), :], partner_of(index, distance, parity))
    index = lax.axis_index("frame")
    if axis == "relay":
        partner = jnp.where(index % 2 == parity, index + distance, index - distance)
    else:
        partner = partner_of(index, distance, parity)
    inside = (partner >= 0) & (partner < lax.axis_size("frame"))
    upper = jnp.where(partner > index, 1, 0)
    entries = partner_flags[distance.bit_length() - 1, pl.ds(upper, 1), :]
    return entry_of(entries, jnp.where(inside, index, -1))


def chosen(flag, one, other):
    return jnp.where(jnp.broadcast_to(flag, one.shape) > 0, one, other)


def key_matrix(key_rows):
    key_high, key_low = halves(key_rows)
    return jnp.concatenate([key_high, key_high, key_low, key_low], axis=1)


def value_matrix(value_rows):
    return jnp.concatenate(halves(value_rows), axis=1)


def query_matrix(query_rows):
    score_scale = math.log2(math.e) / math.sqrt(query_rows.shape[1])
    query_high, query_low = halves(query_rows * score_scale)
    return jnp.concatenate([query_high, query_low, query_high, query_low], axis=1)


def rows_of(kind, refs):
    if kind == "stacked":
        rows = refs[0].shape[0] // 2
        return refs[0][:rows, :], refs[0][rows:, :], 1
    return refs[0][...], refs[1][...], 2


def read_block(kind, which, tables, refs):
    if kind != "either":
        key_rows, value_rows, used = rows_of(kind, refs)
        return key_rows, value_rows, block_flag(which, *tables), used
    position = 0
    key_rows = None
    for one_kind, one in which:
        more_keys, more_values, used = rows_of(one_kind, refs[position:])
        other = block_flag(one, *tables)
        if key_rows is None:
            key_rows, value_rows, flag = more_keys, more_values, other
        else:
            key_rows = chosen(other, more_keys, key_rows)
            value_rows = chosen(other, more_values, value_rows)
            flag = jnp.maximum(flag, other)
        position += used
    return key_rows, value_rows, flag, position


def own_kernel(queries, keys, values, out_max, out_total, out_weighted, stacked, query_parts, staged, sems):
    row_count = queries.shape[0]
    rows = keys.shape[0]
    copies = []
    for source, target, base in ((keys, stacked, 0), (queries, staged, 0), (values, stacked, rows)):
        piece = source.shape[0] // fetch_pieces
        for start in range(0, source.shape[0], piece):
            copy = pltpu.make_async_copy(
                source.at[start : start + piece, :],
                target.at[base + start : base + start + piece, :],
                sems.at[len(copies)],
            )
            copy.start()
            copies.append(copy)
    for copy in copies[: 2 * fetch_pieces]:
        copy.wait()
    key_parts = key_matrix(stacked[:rows, :])
    query_parts[...] = query_matrix(staged[...])
    for copy in copies[2 * fetch_pieces :]:
        copy.wait()
    value_parts = value_matrix(stacked[rows:, :])
    chunk = min(row_chunk, row_count)
    for start in range(0, row_count, chunk):
        part = slice(start, start + chunk)
        running_max, total, weighted = absorb(None, query_parts[part, :], key_parts, value_parts, None)
        out_max[part, :] = jnp.broadcast_to(running_max, (chunk, lane_count))
        out_total[part, :] = total
        out_weighted[part, :] = weighted


def attend_kernel(plan, last, block_mask, partner_flags, query_parts, *refs):
    position = 0
    key_parts = []
    value_parts = []
    enabled = []
    for kind, which in plan:
        key_rows, value_rows, flag, used = read_block(
            kind, which, (block_mask, partner_flags), refs[position:]
        )
        position += used
        key_parts.append(key_matrix(key_rows))
        value_parts.append(value_matrix(value_rows))
        enabled.append(flag)
    carried = refs[position : position + 3]
    outs = refs[position + 3 :]
    row_count = query_parts.shape[0]
    width = carried[2].shape[1] // 2
    chunk = min(row_chunk, row_count)
    copies = []
    for start in range(0, row_count, chunk):
        rows = slice(start, start + chunk)
        state = (carried[0][rows, :1], carried[1][rows, :], carried[2][rows, :])
        for index in range(len(plan)):
            state = absorb(state, query_parts[rows, :], key_parts[index], value_parts[index], enabled[index])
        running_max, total, weighted = state
        if last:
            out, staged, sems = outs
            inverse = 1.0 / jnp.sum(total, axis=1, keepdims=True)
            staged[rows, :] = (weighted[:, :width] + weighted[:, width:]) * inverse
            copy = pltpu.make_async_copy(staged.at[rows, :], out.at[rows, :], sems.at[len(copies)])
            copy.start()
            copies.append(copy)
        else:
            outs[0][rows, :] = jnp.broadcast_to(running_max, (chunk, lane_count))
            outs[1][rows, :] = total
            outs[2][rows, :] = weighted
    for copy in copies:
        copy.wait()


def cost_of(block_count, row_count, width):
    work = block_count * row_count * row_count
    return pl.CostEstimate(
        flops=16 * work * width, bytes_accessed=8 * block_count * row_count * width, transcendentals=work
    )


def state_shapes(row_count, width):
    return tuple(
        jax.ShapeDtypeStruct((row_count, columns), jnp.float32)
        for columns in (lane_count, lane_count, 2 * width)
    )


def attend_own(queries, keys, values):
    row_count, width = queries.shape
    whole = pl.BlockSpec(memory_space=pltpu.VMEM)
    operands = [pltpu.with_memory_space_constraint(array, pltpu.HBM) for array in (queries, keys, values)]
    out_shape = (
        *state_shapes(row_count, width),
        jax.ShapeDtypeStruct((2 * keys.shape[0], width), jnp.float32),
        jax.ShapeDtypeStruct((row_count, 4 * width), jnp.bfloat16),
    )
    *state, stacked, query_parts = pl.pallas_call(
        own_kernel,
        in_specs=[pl.BlockSpec(memory_space=pltpu.HBM)] * 3,
        out_specs=(whole,) * len(out_shape),
        out_shape=out_shape,
        scratch_shapes=[
            pltpu.VMEM((row_count, width), jnp.float32),
            pltpu.SemaphoreType.DMA((3 * fetch_pieces,)),
        ],
        compiler_params=pltpu.CompilerParams(vmem_limit_bytes=kernel_vmem),
        cost_estimate=cost_of(1, row_count, width),
    )(*operands)
    return state, stacked, query_parts


def attend(state, tables, query_parts, blocks, last=False):
    row_count = query_parts.shape[0]
    width = state[2].shape[1] // 2
    plan = tuple((kind, which) for kind, which, _ in blocks)
    arrays = [array for _, _, group in blocks for array in group]
    whole = pl.BlockSpec(memory_space=pltpu.VMEM)
    if last:
        out_shape = jax.ShapeDtypeStruct((row_count, width), jnp.float32)
        out_specs = pl.BlockSpec(memory_space=pl.ANY)
        pieces = row_count // min(row_chunk, row_count)
        scratch = [pltpu.VMEM((row_count, width), jnp.float32), pltpu.SemaphoreType.DMA((pieces,))]
    else:
        out_shape = state_shapes(row_count, width)
        out_specs = (whole,) * len(out_shape)
        scratch = []
    operands = (*tables, query_parts, *arrays, *state)
    return pl.pallas_call(
        functools.partial(attend_kernel, plan, last),
        in_specs=[whole] * len(operands),
        out_specs=out_specs,
        out_shape=out_shape,
        scratch_shapes=scratch,
        compiler_params=pltpu.CompilerParams(vmem_limit_bytes=kernel_vmem),
        cost_estimate=cost_of(len(blocks), row_count, width),
    )(*operands)


def attend_all(state, tables, query_parts, blocks):
    for start in range(0, len(blocks), call_blocks):
        state = attend(state, tables, query_parts, blocks[start : start + call_blocks])
    return state


def matching(size, distance, parity):
    lower = [i for i in range(size - distance) if (i // distance) % 2 == parity]
    return [(i, i + distance) for i in lower] + [(i + distance, i) for i in lower]


def attention(queries, keys, values, block_mask, partner_flags):
    blocks = lax.axis_size("space")
    groups = lax.axis_size("frame")
    levels = partner_flags.shape[1]
    tables = (block_mask, jnp.transpose(partner_flags, (1, 2, 0)))

    near = {}
    for parity in (1, 0):
        route = matching(groups, 1, parity)
        if route:
            near[parity] = (lax.ppermute(keys, "frame", route), lax.ppermute(values, "frame", route))
    near_blocks = [("pair", ("frame", 1, parity), arrays) for parity, arrays in near.items()]

    far_blocks = []
    for parity in (1, 0) if levels > 1 and len(near) == 2 else ():
        holders = {target for _, target in matching(groups, 1, 1 - parity)}
        route = [pair for pair in matching(groups, 1, parity) if pair[0] in holders]
        arrays = (lax.ppermute(near[1 - parity][0], "frame", route), lax.ppermute(near[1 - parity][1], "frame", route))
        far_blocks.append(("pair", ("relay", 2, parity), arrays))

    for level in range(2, levels):
        for parity in (0, 1):
            route = matching(groups, 2**level, parity)
            if route:
                arrays = tuple(lax.ppermute(array, "frame", route) for array in (keys, values))
                far_blocks.append(("pair", ("frame", 2**level, parity), arrays))

    state, stacked, query_parts = attend_own(queries, keys, values)

    window_blocks = []
    for distance in range(1, blocks // 2 + 1):
        for parity in (0, 1):
            route = matching(blocks, distance, parity)
            if route:
                array = lax.ppermute(stacked, "space", route)
                window_blocks.append(("stacked", ("space", distance, parity), (array,)))

    single = len(far_blocks) == 2 and groups <= 2 * far_distance
    final = far_blocks if single else (near_blocks + far_blocks)[-1:]
    sides = [block for block in window_blocks if block[1][2] == 0 and block[1][1] * 2 < blocks]
    rest = [block for block in window_blocks if all(block is not side for side in sides)]
    near_blocks = [block for block in near_blocks if all(block is not other for other in final)]
    far_blocks = [block for block in far_blocks if all(block is not other for other in final)]
    state = attend_all(state, tables, query_parts, sides + near_blocks)
    state = attend_all(state, tables, query_parts, rest)
    state = attend_all(state, tables, query_parts, far_blocks)
    if len(final) > 1:
        which = tuple((kind, one) for kind, one, _ in final)
        final = [("either", which, tuple(array for _, _, group in final for array in group))]
    return attend(state, tables, query_parts, final, last=True)


def solution(mesh):
    rows = P(("groups", "frame", "space"), None)
    return jax.shard_map(attention, mesh=mesh, in_specs=(rows, rows, rows, P(), P()), out_specs=rows, check_vma=False)
```

time: 50.4 us -> 45 us (0.89)
  starting transfers between devices: 15.6 us -> 12.6 us
  local copies, waits for them, and re-layouts: 2.49 us -> 0.68 us
  Pallas kernels: 10.3 us -> 9.04 us
  waiting for transfers between devices: 21.6 us -> 22.2 us
    ppermute x6 -> x4, waiting for transfers between devices: 18.5 us -> 12.5 us  [the longest x2 9.72 us: attention(): lax.ppermute(near[1 - parity][0], 'frame', route)]
    ppermute x2 -> x3, waiting for transfers between devices: 0.01 us -> 4.82 us  [attention(): array = lax.ppermute(stacked, 'space', route)]
    ppermute x2, starting transfers between devices: 5.13 us -> 0.74 us  [attention(): lax.ppermute(values, 'frame', route)]
    ppermute x2 -> x3, starting transfers between devices: 0.82 us -> 4.16 us  [attention(): array = lax.ppermute(stacked, 'space', route)]
    ppermute x6 -> x4, starting transfers between devices: 5.93 us -> 3.94 us  [the longest x2 1.97 us: attention(): lax.ppermute(near[1 - parity][1], 'frame', route)]
    pallas_call x4, Pallas kernels: 10.3 us -> 9.04 us  [the longest x3 6.63 us: attend(): pl.pallas_call(functools.partial(attend_kernel, plan, last), in_specs=[wh...]
    unnamed x12 -> x8, local copies, waits for them, and re-layouts: 1.79 us -> 0.68 us
    ppermute x2, waiting for transfers between devices: 3.1 us -> 4.09 us  [attention(): lax.ppermute(values, 'frame', route)]
  transfers between devices with their start and end apart: 12 -> 11, of which waited for: 5 -> 5; matrix products, arithmetic and copies ran while one was open for 5% -> 0% of each run, Pallas kernels for 15% -> 16%
where the time goes in v2:
time: 45 us; the launch traced here: 44.6 us
  waiting for transfers between devices  22.2 us (49%)
  starting transfers between devices  12.6 us (28%)
  Pallas kernels  9.04 us (20%)
  local copies, waits for them, and re-layouts  0.68 us (2%)
    ppermute x2, waiting for transfers between devices, attention(): lax.ppermute(near[1 - parity][0], 'frame', route)  9.72 us
    pallas_call x3, Pallas kernels, attend(): pl.pallas_call(functools.partial(attend_kernel, plan, last), in_specs=[wh...  6.63 us
    ppermute x3, waiting for transfers between devices, attention(): array = lax.ppermute(stacked, 'space', route)  4.82 us
    ppermute x3, starting transfers between devices, attention(): array = lax.ppermute(stacked, 'space', route)  4.16 us
    ppermute x2, waiting for transfers between devices, attention(): lax.ppermute(values, 'frame', route)  4.09 us
    ppermute x2, starting transfers between devices, attention(): lax.ppermute(keys, 'frame', route)  3.72 us
    ppermute x2, waiting for transfers between devices, attention(): lax.ppermute(near[1 - parity][1], 'frame', route)  2.81 us
    pallas_call x1, Pallas kernels, attend_own(): pl.pallas_call(own_kernel, in_specs=[pl.BlockSpec(memory_space=pltpu.HBM)...  2.42 us
  transfers between devices with their start and end apart: 11, of which 5 were waited for; matrix products, arithmetic and copies ran while one was open for 0% of the time, Pallas kernels for 16%

profile of v2, /device:TPU:0, one launch (start us, length us, event | category | flops | bytes accessed | tf_op | source)
XLA Modules:
  0.0 44.6 jit_solution(16438090412919224428)
XLA Ops:
  0.0 0.0 copy-start.2
  0.0 0.0 copy-start.3
  0.0 3.1 %collective-permute-start = (f32[512,128]{1,0:T(8,128)}, f32[512,128]{1,0:T(8,128)S(1)}, u32[]{:S(2)}, u32[]{:S(2)}) collective-permute-start(f32[512,128]{1,0:T(8,128)} %keys.1), channel_id=1, source_target_pairs={{0,4},{8,12},{4,0},{12,8},{1,5},{9,13},{5,1},{13,9},{2,6},{10,14},... | collective-permute-start | bytes 786440 | tf_op jit(solution)/shard_map/ppermute | solution.py:279
  3.1 0.1 collective-permute-start.2
  3.1 0.0 copy-start.1
  3.1 2.4 %shard_map.55 = (f32[512,128]{1,0:T(8,128)S(1)}, f32[512,128]{1,0:T(8,128)S(1)}, f32[512,256]{1,0:T(8,128)S(1)}, f32[1024,128]{1,0:T(8,128)S(1)}, bf16[512,512]{1,0:T(8,128)(2,1)S(1)}) custom-call(f32[512,128]{1,0:T(8,128)} %queries.1, f32[512,128]{1,0:T(8,128)} %keys.1, f32[512,128]{1,0:T(8,128)} %values.1), custom_call_target="tpu_custom_call" | custom-call | flops 536870912 | bytes 524288 | tf_op jit(solution)/shard_map/pallas_call | solution.py:216
  5.6 0.1 collective-permute-start.10
  5.6 0.7 %collective-permute-start.8 = (f32[1024,128]{1,0:T(8,128)S(1)}, f32[1024,128]{1,0:T(8,128)S(1)}, u32[]{:S(2)}, u32[]{:S(2)}) collective-permute-start(f32[1024,128]{1,0:T(8,128)S(1)} %get-tuple-element.17), channel_id=1, source_target_pairs={{1,2},{2,1},{5,6},{6,5},{9,10},{10,9},{13,14},{14,13},{17,18},{18,... | collective-permute-start | bytes 1572872 | tf_op jit(solution)/shard_map/ppermute | solution.py:303
  6.3 3.4 %collective-permute-start.9 = (f32[1024,128]{1,0:T(8,128)S(1)}, f32[1024,128]{1,0:T(8,128)S(1)}, u32[]{:S(2)}, u32[]{:S(2)}) collective-permute-start(f32[1024,128]{1,0:T(8,128)S(1)} %get-tuple-element.17), channel_id=1, source_target_pairs={{0,2},{1,3},{2,0},{3,1},{4,6},{5,7},{6,4},{7,5},{8,10},{9,11},{10,... | collective-permute-start | bytes 1572872 | tf_op jit(solution)/shard_map/ppermute | solution.py:303
  9.7 0.8 %collective-permute-done.refs_3_ = f32[512,128]{1,0:T(8,128)S(1)} collective-permute-done((f32[512,128]{1,0:T(8,128)}, f32[512,128]{1,0:T(8,128)S(1)}, u32[]{:S(2)}, u32[]{:S(2)}) %collective-permute-start) | collective-permute-done | bytes 262176 | tf_op jit(solution)/shard_map/ppermute | solution.py:279
  10.5 0.0 copy-done.2
  10.5 0.7 %collective-permute-start.4 = (f32[512,128]{1,0:T(8,128)S(1)}, f32[512,128]{1,0:T(8,128)S(1)}, u32[]{:S(2)}, u32[]{:S(2)}) collective-permute-start(f32[512,128]{1,0:T(8,128)S(1)} %copy-done.2), channel_id=1, source_target_pairs={{4,8},{8,4},{5,9},{9,5},{6,10},{10,6},{7,11},{11,7},{20,24},{24,20... | collective-permute-start | bytes 786440 | tf_op jit(solution)/shard_map/ppermute | solution.py:279
  11.2 4.1 %collective-permute-done.2.refs_4_ = f32[512,128]{1,0:T(8,128)S(1)} collective-permute-done((f32[512,128]{1,0:T(8,128)}, f32[512,128]{1,0:T(8,128)S(1)}, u32[]{:S(2)}, u32[]{:S(2)}) %collective-permute-start.2) | collective-permute-done | bytes 262176 | tf_op jit(solution)/shard_map/ppermute | solution.py:279
  15.3 0.0 copy-done.3
  15.3 0.7 %collective-permute-start.6 = (f32[512,128]{1,0:T(8,128)S(1)}, f32[512,128]{1,0:T(8,128)S(1)}, u32[]{:S(2)}, u32[]{:S(2)}) collective-permute-start(f32[512,128]{1,0:T(8,128)S(1)} %copy-done.3), channel_id=1, source_target_pairs={{4,8},{8,4},{5,9},{9,5},{6,10},{10,6},{7,11},{11,7},{20,24},{24,20... | collective-permute-start | bytes 786440 | tf_op jit(solution)/shard_map/ppermute | solution.py:279
  15.9 0.0 collective-permute-done.4.refs_1_
  15.9 0.7 %collective-permute-start.1 = (f32[512,128]{1,0:T(8,128)S(1)}, f32[512,128]{1,0:T(8,128)S(1)}, u32[]{:S(2)}, u32[]{:S(2)}) collective-permute-start(f32[512,128]{1,0:T(8,128)S(1)} %collective-permute-done.refs_3_), channel_id=1, source_target_pairs={{4,8},{8,4},{5,9},{9,5},{6,10},{10,6},{7,11},{11,7},{20,24},{24,20... | collective-permute-start | bytes 786440 | tf_op jit(solution)/shard_map/ppermute | solution.py:286
  16.6 0.0 collective-permute-done.6.refs_2_
  16.6 0.7 %collective-permute-start.3 = (f32[512,128]{1,0:T(8,128)S(1)}, f32[512,128]{1,0:T(8,128)S(1)}, u32[]{:S(2)}, u32[]{:S(2)}) collective-permute-start(f32[512,128]{1,0:T(8,128)S(1)} %collective-permute-done.2.refs_4_), channel_id=1, source_target_pairs={{4,8},{8,4},{5,9},{9,5},{6,10},{10,6},{7,11},{11,7},{20,24},{24,20... | collective-permute-start | bytes 786440 | tf_op jit(solution)/shard_map/ppermute | solution.py:286
  17.3 0.0 collective-permute-done.10.refs_0_
  17.3 1.3 %collective-permute-start.5 = (f32[512,128]{1,0:T(8,128)S(1)}, f32[512,128]{1,0:T(8,128)S(1)}, u32[]{:S(2)}, u32[]{:S(2)}) collective-permute-start(f32[512,128]{1,0:T(8,128)S(1)} %collective-permute-done.4.refs_1_), channel_id=1, source_target_pairs={{8,12},{4,0},{9,13},{5,1},{10,14},{6,2},{11,15},{7,3},{24,28},{20,... | collective-permute-start | bytes 786440 | tf_op jit(solution)/shard_map/ppermute | solution.py:286
  18.6 0.0 collective-permute-done.8.refs_0_
  18.6 1.3 %collective-permute-start.7 = (f32[512,128]{1,0:T(8,128)S(1)}, f32[512,128]{1,0:T(8,128)S(1)}, u32[]{:S(2)}, u32[]{:S(2)}) collective-permute-start(f32[512,128]{1,0:T(8,128)S(1)} %collective-permute-done.6.refs_2_), channel_id=1, source_target_pairs={{8,12},{4,0},{9,13},{5,1},{10,14},{6,2},{11,15},{7,3},{24,28},{20,... | collective-permute-start | bytes 786440 | tf_op jit(solution)/shard_map/ppermute | solution.py:286
  19.9 0.0 copy-start
  20.0 0.0 copy-done.1
  20.0 0.7 %copy-done = s32[4,4]{1,0:T(4,128)S(1)} copy-done((s32[4,4]{1,0:T(4,128)S(1)}, s32[4,4]{1,0:T(4,128)}, u32[]{:S(2)}) %copy-start) | copy-done | bytes 88
  20.6 2.6 %shard_map.56 = (f32[512,128]{1,0:T(8,128)S(1)}, f32[512,128]{1,0:T(8,128)S(1)}, f32[512,256]{1,0:T(8,128)S(1)}) custom-call(s32[4,4]{1,0:T(4,128)S(1)} %copy-done, s32[2,2,4]{2,1,0:T(2,128)S(1)} %bitcast.1, bf16[512,512]{1,0:T(8,128)(2,1)S(1)} %get-tuple-element.16.query_parts, f32[1024,128]{1,0:T(8,128)S(1)} %collective-permute-done.10.refs_0_, ...), custom_call_target="tpu_custom_call" | custom-call | flops 1610612736 | bytes 1572864 | tf_op jit(solution)/shard_map/pallas_call | solution.py:247
  23.2 4.8 %collective-permute-done.9.refs_1_ = f32[1024,128]{1,0:T(8,128)S(1)} collective-permute-done((f32[1024,128]{1,0:T(8,128)S(1)}, f32[1024,128]{1,0:T(8,128)S(1)}, u32[]{:S(2)}, u32[]{:S(2)}) %collective-permute-start.9) | collective-permute-done | bytes 524320 | tf_op jit(solution)/shard_map/ppermute | solution.py:303
  28.0 2.0 %shard_map.57 = (f32[512,128]{1,0:T(8,128)S(1)}, f32[512,128]{1,0:T(8,128)S(1)}, f32[512,256]{1,0:T(8,128)S(1)}) custom-call(s32[4,4]{1,0:T(4,128)S(1)} %copy-done, s32[2,2,4]{2,1,0:T(2,128)S(1)} %bitcast.2, bf16[512,512]{1,0:T(8,128)(2,1)S(1)} %get-tuple-element.16.query_parts, f32[1024,128]{1,0:T(8,128)S(1)} %collective-permute-done.8.refs_0_, ...), custom_call_target="tpu_custom_call" | custom-call | flops 1073741824 | bytes 1048576 | tf_op jit(solution)/shard_map/pallas_call | solution.py:247
  30.0 0.0 collective-permute-done.1.refs_0_
  30.0 0.0 collective-permute-done.3.refs_1_
  30.0 9.7 %collective-permute-done.5.refs_2_ = f32[512,128]{1,0:T(8,128)S(1)} collective-permute-done((f32[512,128]{1,0:T(8,128)S(1)}, f32[512,128]{1,0:T(8,128)S(1)}, u32[]{:S(2)}, u32[]{:S(2)}) %collective-permute-start.5) | collective-permute-done | bytes 262176 | tf_op jit(solution)/shard_map/ppermute | solution.py:286
  39.8 2.8 %collective-permute-done.7.refs_3_ = f32[512,128]{1,0:T(8,128)S(1)} collective-permute-done((f32[512,128]{1,0:T(8,128)S(1)}, f32[512,128]{1,0:T(8,128)S(1)}, u32[]{:S(2)}, u32[]{:S(2)}) %collective-permute-start.7) | collective-permute-done | bytes 262176 | tf_op jit(solution)/shard_map/ppermute | solution.py:286
  42.6 2.1 %shard_map.58 = f32[512,128]{1,0:T(8,128)} custom-call(s32[4,4]{1,0:T(4,128)S(1)} %copy-done, s32[2,2,4]{2,1,0:T(2,128)S(1)} %bitcast.3, bf16[512,512]{1,0:T(8,128)(2,1)S(1)} %get-tuple-element.16.query_parts, f32[512,128]{1,0:T(8,128)S(1)} %collective-permute-done.1.refs_0_, f32[512,128]{1,0:T(8,128)S(1)} %collective-permute-done.3.refs_1_, ...), custom_call_target="tpu_custom_call" | custom-call | flops 536870912 | bytes 524288 | tf_op jit(solution)/shard_map/pallas_call | solution.py:247
Async XLA Ops:
  0.0 10.5 %copy-start.2 = (f32[512,128]{1,0:T(8,128)S(1)}, f32[512,128]{1,0:T(8,128)}, u32[]{:S(2)}) copy-start(f32[512,128]{1,0:T(8,128)} %keys.1) | copy-start | bytes 786436
  0.0 15.3 %copy-start.3 = (f32[512,128]{1,0:T(8,128)S(1)}, f32[512,128]{1,0:T(8,128)}, u32[]{:S(2)}) copy-start(f32[512,128]{1,0:T(8,128)} %values.1) | copy-start | bytes 786436
  0.0 10.5 %collective-permute-start = (f32[512,128]{1,0:T(8,128)}, f32[512,128]{1,0:T(8,128)S(1)}, u32[]{:S(2)}, u32[]{:S(2)}) collective-permute-start(f32[512,128]{1,0:T(8,128)} %keys.1), channel_id=1, source_target_pairs={{0,4},{8,12},{4,0},{12,8},{1,5},{9,13},{5,1},{13,9},{2,6},{10,14},... | collective-permute-start | bytes 786440 | tf_op jit(solution)/shard_map/ppermute | solution.py:279
  3.1 12.2 %collective-permute-start.2 = (f32[512,128]{1,0:T(8,128)}, f32[512,128]{1,0:T(8,128)S(1)}, u32[]{:S(2)}, u32[]{:S(2)}) collective-permute-start(f32[512,128]{1,0:T(8,128)} %values.1), channel_id=1, source_target_pairs={{0,4},{8,12},{4,0},{12,8},{1,5},{9,13},{5,1},{13,9},{2,6},{10,14},... | collective-permute-start | bytes 786440 | tf_op jit(solution)/shard_map/ppermute | solution.py:279
  3.1 16.8 %copy-start.1 = (s32[4,2,2]{0,2,1:T(2,128)S(1)}, s32[4,2,2]{0,2,1:T(2,128)}, u32[]{:S(2)}) copy-start(s32[4,2,2]{0,2,1:T(2,128)} %param.9) | copy-start | bytes 196
  5.6 11.8 %collective-permute-start.10 = (f32[1024,128]{1,0:T(8,128)S(1)}, f32[1024,128]{1,0:T(8,128)S(1)}, u32[]{:S(2)}, u32[]{:S(2)}) collective-permute-start(f32[1024,128]{1,0:T(8,128)S(1)} %get-tuple-element.17), channel_id=1, source_target_pairs={{0,1},{2,3},{1,0},{3,2},{4,5},{6,7},{5,4},{7,6},{8,9},{10,11},{9,8... | collective-permute-start | bytes 1572872 | tf_op jit(solution)/shard_map/ppermute | solution.py:303
  5.6 13.0 %collective-permute-start.8 = (f32[1024,128]{1,0:T(8,128)S(1)}, f32[1024,128]{1,0:T(8,128)S(1)}, u32[]{:S(2)}, u32[]{:S(2)}) collective-permute-start(f32[1024,128]{1,0:T(8,128)S(1)} %get-tuple-element.17), channel_id=1, source_target_pairs={{1,2},{2,1},{5,6},{6,5},{9,10},{10,9},{13,14},{14,13},{17,18},{18,... | collective-permute-start | bytes 1572872 | tf_op jit(solution)/shard_map/ppermute | solution.py:303
  6.3 21.7 %collective-permute-start.9 = (f32[1024,128]{1,0:T(8,128)S(1)}, f32[1024,128]{1,0:T(8,128)S(1)}, u32[]{:S(2)}, u32[]{:S(2)}) collective-permute-start(f32[1024,128]{1,0:T(8,128)S(1)} %get-tuple-element.17), channel_id=1, source_target_pairs={{0,2},{1,3},{2,0},{3,1},{4,6},{5,7},{6,4},{7,5},{8,10},{9,11},{10,... | collective-permute-start | bytes 1572872 | tf_op jit(solution)/shard_map/ppermute | solution.py:303
  10.5 5.4 %collective-permute-start.4 = (f32[512,128]{1,0:T(8,128)S(1)}, f32[512,128]{1,0:T(8,128)S(1)}, u32[]{:S(2)}, u32[]{:S(2)}) collective-permute-start(f32[512,128]{1,0:T(8,128)S(1)} %copy-done.2), channel_id=1, source_target_pairs={{4,8},{8,4},{5,9},{9,5},{6,10},{10,6},{7,11},{11,7},{20,24},{24,20... | collective-permute-start | bytes 786440 | tf_op jit(solution)/shard_map/ppermute | solution.py:279
  15.3 1.4 %collective-permute-start.6 = (f32[512,128]{1,0:T(8,128)S(1)}, f32[512,128]{1,0:T(8,128)S(1)}, u32[]{:S(2)}, u32[]{:S(2)}) collective-permute-start(f32[512,128]{1,0:T(8,128)S(1)} %copy-done.3), channel_id=1, source_target_pairs={{4,8},{8,4},{5,9},{9,5},{6,10},{10,6},{7,11},{11,7},{20,24},{24,20... | collective-permute-start | bytes 786440 | tf_op jit(solution)/shard_map/ppermute | solution.py:279
  15.9 14.1 %collective-permute-start.1 = (f32[512,128]{1,0:T(8,128)S(1)}, f32[512,128]{1,0:T(8,128)S(1)}, u32[]{:S(2)}, u32[]{:S(2)}) collective-permute-start(f32[512,128]{1,0:T(8,128)S(1)} %collective-permute-done.refs_3_), channel_id=1, source_target_pairs={{4,8},{8,4},{5,9},{9,5},{6,10},{10,6},{7,11},{11,7},{20,24},{24,20... | collective-permute-start | bytes 786440 | tf_op jit(solution)/shard_map/ppermute | solution.py:286
  16.6 13.4 %collective-permute-start.3 = (f32[512,128]{1,0:T(8,128)S(1)}, f32[512,128]{1,0:T(8,128)S(1)}, u32[]{:S(2)}, u32[]{:S(2)}) collective-permute-start(f32[512,128]{1,0:T(8,128)S(1)} %collective-permute-done.2.refs_4_), channel_id=1, source_target_pairs={{4,8},{8,4},{5,9},{9,5},{6,10},{10,6},{7,11},{11,7},{20,24},{24,20... | collective-permute-start | bytes 786440 | tf_op jit(solution)/shard_map/ppermute | solution.py:286
  17.3 22.4 %collective-permute-start.5 = (f32[512,128]{1,0:T(8,128)S(1)}, f32[512,128]{1,0:T(8,128)S(1)}, u32[]{:S(2)}, u32[]{:S(2)}) collective-permute-start(f32[512,128]{1,0:T(8,128)S(1)} %collective-permute-done.4.refs_1_), channel_id=1, source_target_pairs={{8,12},{4,0},{9,13},{5,1},{10,14},{6,2},{11,15},{7,3},{24,28},{20,... | collective-permute-start | bytes 786440 | tf_op jit(solution)/shard_map/ppermute | solution.py:286
  18.6 23.9 %collective-permute-start.7 = (f32[512,128]{1,0:T(8,128)S(1)}, f32[512,128]{1,0:T(8,128)S(1)}, u32[]{:S(2)}, u32[]{:S(2)}) collective-permute-start(f32[512,128]{1,0:T(8,128)S(1)} %collective-permute-done.6.refs_2_), channel_id=1, source_target_pairs={{8,12},{4,0},{9,13},{5,1},{10,14},{6,2},{11,15},{7,3},{24,28},{20,... | collective-permute-start | bytes 786440 | tf_op jit(solution)/shard_map/ppermute | solution.py:286
  19.9 0.7 %copy-start = (s32[4,4]{1,0:T(4,128)S(1)}, s32[4,4]{1,0:T(4,128)}, u32[]{:S(2)}) copy-start(s32[4,4]{1,0:T(4,128)} %block_mask.5) | copy-start | bytes 196

commit v3 on v2

v3 whole, which is shorter than its diff:
```python
import functools
import math

import jax
import jax.numpy as jnp
from jax import lax
from jax.experimental import pallas as pl
from jax.experimental.pallas import tpu as pltpu
from jax.sharding import PartitionSpec as P


masked_score = -1e30
lane_count = 128
row_chunk = 256
call_blocks = 4
kernel_vmem = 24 * 2**20
fetch_pieces = 4
write_pieces = 4
far_distance = 2


def halves(x):
    high = x.astype(jnp.bfloat16)
    return high, (x - high.astype(jnp.float32)).astype(jnp.bfloat16)


def fold_lanes(x, op):
    folded = x[:, :lane_count]
    for start in range(lane_count, x.shape[1], lane_count):
        folded = op(folded, x[:, start : start + lane_count])
    return folded


def absorb(state, query_parts, key_parts, value_parts, enabled):
    scores = lax.dot_general(
        query_parts, key_parts, (((1,), (1,)), ((), ())), preferred_element_type=jnp.float32
    )
    block_max = jnp.max(fold_lanes(scores, jnp.maximum), axis=1, keepdims=True)
    if enabled is not None:
        block_max = chosen(enabled, block_max, jnp.full_like(block_max, masked_score))
    new_max = block_max if state is None else jnp.maximum(state[0], block_max)
    shift = new_max if enabled is None else chosen(enabled, new_max, jnp.full_like(new_max, -masked_score))
    weights = jnp.exp2(scores - shift)
    total = fold_lanes(weights, jnp.add)
    weights_high, weights_low = halves(weights)
    weighted = jnp.dot(weights_high, value_parts, preferred_element_type=jnp.float32)
    weighted += jnp.dot(weights_low, value_parts, preferred_element_type=jnp.float32)
    if state is None:
        return new_max, total, weighted
    factor = jnp.exp2(state[0] - new_max)
    return new_max, state[1] * factor + total, state[2] * factor + weighted


def partner_of(index, distance, parity):
    return jnp.where((index // distance) % 2 == parity, index + distance, index - distance)


def entry_of(entries, column):
    columns = lax.broadcasted_iota(jnp.int32, entries.shape, 1)
    return jnp.sum(jnp.where(columns == column, entries, 0).astype(jnp.float32), axis=1, keepdims=True)


def block_flag(which, block_mask, partner_flags):
    axis, distance, parity = which
    if axis == "space":
        index = lax.axis_index("space")
        return entry_of(block_mask[pl.ds(index, 1), :], partner_of(index, distance, parity))
    index = lax.axis_index("frame")
    if axis == "relay":
        partner = jnp.where(index % 2 == parity, index + distance, index - distance)
    else:
        partner = partner_of(index, distance, parity)
    inside = (partner >= 0) & (partner < lax.axis_size("frame"))
    upper = jnp.where(partner > index, 1, 0)
    entries = partner_flags[distance.bit_length() - 1, pl.ds(upper, 1), :]
    return entry_of(entries, jnp.where(inside, index, -1))


def chosen(flag, one, other):
    return jnp.where(jnp.broadcast_to(flag, one.shape) > 0, one, other)


def key_matrix(key_rows):
    key_high, key_low = halves(key_rows)
    return jnp.concatenate([key_high, key_high, key_low, key_low], axis=1)


def value_matrix(value_rows):
    return jnp.concatenate(halves(value_rows), axis=1)


def query_matrix(query_rows):
    score_scale = math.log2(math.e) / math.sqrt(query_rows.shape[1])
    query_high, query_low = halves(query_rows * score_scale)
    return jnp.concatenate([query_high, query_low, query_high, query_low], axis=1)


def fetch_kernel(block_mask, partner_flags, queries, keys, values, stacked, query_copy, mask_copy, flags_copy, sems):
    rows = keys.shape[0]
    copies = []
    for source, target, base in ((keys, stacked, 0), (values, stacked, rows), (queries, query_copy, 0)):
        piece = source.shape[0] // fetch_pieces
        for start in range(0, source.shape[0], piece):
            copies.append(
                pltpu.make_async_copy(
                    source.at[start : start + piece, :],
                    target.at[base + start : base + start + piece, :],
                    sems.at[len(copies)],
                )
            )
    for source, target in ((block_mask, mask_copy), (partner_flags, flags_copy)):
        copies.append(pltpu.make_async_copy(source, target, sems.at[len(copies)]))
    for copy in copies:
        copy.start()
    for copy in copies:
        copy.wait()


def own_kernel(queries, stacked, out_max, out_total, out_weighted, query_parts):
    row_count = queries.shape[0]
    rows = stacked.shape[0] // 2
    key_parts = key_matrix(stacked[:rows, :])
    value_parts = value_matrix(stacked[rows:, :])
    chunk = min(row_chunk, row_count)
    for start in range(0, row_count, chunk):
        part = slice(start, start + chunk)
        query_chunk = query_matrix(queries[part, :])
        query_parts[part, :] = query_chunk
        running_max, total, weighted = absorb(None, query_chunk, key_parts, value_parts, None)
        out_max[part, :] = jnp.broadcast_to(running_max, (chunk, lane_count))
        out_total[part, :] = total
        out_weighted[part, :] = weighted


def read_blocks(plan, refs, tables):
    position = 0
    parts = []
    for kind, which in plan:
        if kind == "stacked":
            rows = refs[position].shape[0] // 2
            key_rows, value_rows = refs[position][:rows, :], refs[position][rows:, :]
            position += 1
        else:
            key_rows, value_rows = refs[position][...], refs[position + 1][...]
            position += 2
        parts.append((key_matrix(key_rows), value_matrix(value_rows), block_flag(which, *tables)))
    return parts, position


def attend_kernel(plan, block_mask, partner_flags, query_parts, *refs):
    parts, position = read_blocks(plan, refs, (block_mask, partner_flags))
    old_max, old_total, old_weighted, out_max, out_total, out_weighted = refs[position:]
    row_count = query_parts.shape[0]
    chunk = min(row_chunk, row_count)
    for start in range(0, row_count, chunk):
        rows = slice(start, start + chunk)
        state = (old_max[rows, :1], old_total[rows, :], old_weighted[rows, :])
        for part in parts:
            state = absorb(state, query_parts[rows, :], *part)
        running_max, total, weighted = state
        out_max[rows, :] = jnp.broadcast_to(running_max, (chunk, lane_count))
        out_total[rows, :] = total
        out_weighted[rows, :] = weighted


def brought(whiches, arrays, tables):
    rows = arrays[0][...]
    flag = block_flag(whiches[0], *tables)
    for which, array in zip(whiches[1:], arrays[1:]):
        other = block_flag(which, *tables)
        rows = chosen(other, array[...], rows)
        flag = jnp.maximum(flag, other)
    return rows, flag


def weigh_kernel(plan, whiches, block_mask, partner_flags, query_parts, *refs):
    tables = (block_mask, partner_flags)
    parts, position = read_blocks(plan, refs, tables)
    refs = refs[position:]
    count = len(whiches)
    key_rows, flag = brought(whiches, refs[:count], tables)
    old_max, old_total, old_weighted, out_high, out_low, out_inverse, out_weighted = refs[count:]
    key_parts = key_matrix(key_rows)
    row_count = query_parts.shape[0]
    width = key_rows.shape[1]
    chunk = min(row_chunk, row_count)
    for start in range(0, row_count, chunk):
        rows = slice(start, start + chunk)
        state = (old_max[rows, :1], old_total[rows, :], old_weighted[rows, :])
        for part in parts:
            state = absorb(state, query_parts[rows, :], *part)
        before, total, weighted = state
        scores = lax.dot_general(
            query_parts[rows, :],
            key_parts,
            (((1,), (1,)), ((), ())),
            preferred_element_type=jnp.float32,
        )
        block_max = jnp.max(fold_lanes(scores, jnp.maximum), axis=1, keepdims=True)
        block_max = chosen(flag, block_max, jnp.full_like(block_max, masked_score))
        new_max = jnp.maximum(before, block_max)
        factor = jnp.exp2(before - new_max)
        weights = jnp.exp2(scores - chosen(flag, new_max, jnp.full_like(new_max, -masked_score)))
        total = total * factor + fold_lanes(weights, jnp.add)
        inverse = 1.0 / jnp.sum(total, axis=1, keepdims=True)
        out_high[rows, :], out_low[rows, :] = halves(weights)
        out_inverse[rows, :] = jnp.broadcast_to(inverse, (chunk, lane_count))
        out_weighted[rows, :] = (weighted[:, :width] + weighted[:, width:]) * (factor * inverse)


def finish_kernel(whiches, block_mask, partner_flags, *refs):
    count = len(whiches)
    value_rows, _ = brought(whiches, refs[:count], (block_mask, partner_flags))
    weights_high, weights_low, inverse, weighted, out, staged, sems = refs[count:]
    value_parts = value_matrix(value_rows)
    row_count, width = weighted.shape
    chunk = row_count // write_pieces
    copies = []
    for start in range(0, row_count, chunk):
        rows = slice(start, start + chunk)
        more = jnp.dot(weights_high[rows, :], value_parts, preferred_element_type=jnp.float32)
        more += jnp.dot(weights_low[rows, :], value_parts, preferred_element_type=jnp.float32)
        staged[rows, :] = weighted[rows, :] + (more[:, :width] + more[:, width:]) * inverse[rows, :]
        copy = pltpu.make_async_copy(staged.at[rows, :], out.at[rows, :], sems.at[len(copies)])
        copy.start()
        copies.append(copy)
    for copy in copies:
        copy.wait()


def cost_of(block_count, row_count, width):
    work = block_count * row_count * row_count
    return pl.CostEstimate(
        flops=16 * work * width, bytes_accessed=8 * block_count * row_count * width, transcendentals=work
    )


def state_shapes(row_count, width):
    return tuple(
        jax.ShapeDtypeStruct((row_count, columns), jnp.float32)
        for columns in (lane_count, lane_count, 2 * width)
    )


def fetch(tables, queries, keys, values):
    rows, width = keys.shape
    whole = pl.BlockSpec(memory_space=pltpu.VMEM)
    operands = [
        pltpu.with_memory_space_constraint(array, pltpu.HBM) for array in (*tables, queries, keys, values)
    ]
    out_shape = (
        jax.ShapeDtypeStruct((2 * rows, width), keys.dtype),
        jax.ShapeDtypeStruct(queries.shape, queries.dtype),
        *(jax.ShapeDtypeStruct(table.shape, table.dtype) for table in tables),
    )
    stacked, query_copy, *tables = pl.pallas_call(
        fetch_kernel,
        in_specs=[pl.BlockSpec(memory_space=pltpu.HBM)] * len(operands),
        out_specs=(whole,) * len(out_shape),
        out_shape=out_shape,
        scratch_shapes=[pltpu.SemaphoreType.DMA((3 * fetch_pieces + len(tables),))],
        compiler_params=pltpu.CompilerParams(vmem_limit_bytes=kernel_vmem),
    )(*operands)
    return stacked, query_copy, tables


def attend_own(queries, stacked):
    row_count, width = queries.shape
    whole = pl.BlockSpec(memory_space=pltpu.VMEM)
    *state, query_parts = pl.pallas_call(
        own_kernel,
        in_specs=[whole] * 2,
        out_specs=(whole,) * 4,
        out_shape=(
            *state_shapes(row_count, width),
            jax.ShapeDtypeStruct((row_count, 4 * width), jnp.bfloat16),
        ),
        compiler_params=pltpu.CompilerParams(vmem_limit_bytes=kernel_vmem),
        cost_estimate=cost_of(1, row_count, width),
    )(queries, stacked)
    return state, query_parts


def attend(state, tables, query_parts, blocks):
    row_count = query_parts.shape[0]
    width = state[2].shape[1] // 2
    plan = tuple((kind, which) for kind, which, _ in blocks)
    arrays = [array for _, _, group in blocks for array in group]
    whole = pl.BlockSpec(memory_space=pltpu.VMEM)
    operands = (*tables, query_parts, *arrays, *state)
    return pl.pallas_call(
        functools.partial(attend_kernel, plan),
        in_specs=[whole] * len(operands),
        out_specs=(whole,) * 3,
        out_shape=state_shapes(row_count, width),
        compiler_params=pltpu.CompilerParams(vmem_limit_bytes=kernel_vmem),
        cost_estimate=cost_of(len(blocks), row_count, width),
    )(*operands)


def finish(state, tables, query_parts, others, blocks):
    row_count = query_parts.shape[0]
    width = state[2].shape[1] // 2
    whiches = tuple(which for _, which, _ in blocks)
    key_arrays = [keys for _, _, (keys, _) in blocks]
    value_arrays = [values for _, _, (_, values) in blocks]
    whole = pl.BlockSpec(memory_space=pltpu.VMEM)
    arrays = [array for _, _, group in others for array in group]
    plan = tuple((kind, which) for kind, which, _ in others)
    operands = (*tables, query_parts, *arrays, *key_arrays, *state)
    weights = jax.ShapeDtypeStruct((row_count, key_arrays[0].shape[0]), jnp.bfloat16)
    weighed = pl.pallas_call(
        functools.partial(weigh_kernel, plan, whiches),
        in_specs=[whole] * len(operands),
        out_specs=(whole,) * 4,
        out_shape=(
            weights,
            weights,
            jax.ShapeDtypeStruct((row_count, lane_count), jnp.float32),
            jax.ShapeDtypeStruct((row_count, width), jnp.float32),
        ),
        compiler_params=pltpu.CompilerParams(vmem_limit_bytes=kernel_vmem),
        cost_estimate=cost_of(1 + len(others), row_count, width),
    )(*operands)
    operands = (*tables, *value_arrays, *weighed)
    return pl.pallas_call(
        functools.partial(finish_kernel, whiches),
        in_specs=[whole] * len(operands),
        out_specs=pl.BlockSpec(memory_space=pl.ANY),
        out_shape=jax.ShapeDtypeStruct((row_count, width), jnp.float32),
        scratch_shapes=[
            pltpu.VMEM((row_count, width), jnp.float32),
            pltpu.SemaphoreType.DMA((write_pieces,)),
        ],
        compiler_params=pltpu.CompilerParams(vmem_limit_bytes=kernel_vmem),
        cost_estimate=cost_of(1, row_count, width),
    )(*operands)


def attend_all(state, tables, query_parts, blocks):
    for start in range(0, len(blocks), call_blocks):
        state = attend(state, tables, query_parts, blocks[start : start + call_blocks])
    return state


def matching(size, distance, parity):
    lower = [i for i in range(size - distance) if (i // distance) % 2 == parity]
    return [(i, i + distance) for i in lower] + [(i + distance, i) for i in lower]


def through_half(route, size):
    half = size // 2
    pairs = []
    for block, target in route:
        holder = block - half if block >= half else block + half
        if holder == target or abs(holder - target) > abs(block - target):
            return None
        pairs.append((holder, target))
    return pairs if len({holder for holder, _ in pairs}) == len(pairs) else None


def attention(queries, keys, values, block_mask, partner_flags):
    blocks = lax.axis_size("space")
    groups = lax.axis_size("frame")
    levels = partner_flags.shape[1]
    tables = (block_mask, jnp.transpose(partner_flags, (1, 2, 0)))

    near = {}
    for parity in (1, 0):
        route = matching(groups, 1, parity)
        if route:
            near[parity] = (lax.ppermute(keys, "frame", route), lax.ppermute(values, "frame", route))
    near_blocks = [("pair", ("frame", 1, parity), arrays) for parity, arrays in near.items()]

    far_blocks = []
    for parity in (1, 0) if levels > 1 and len(near) == 2 else ():
        holders = {target for _, target in matching(groups, 1, 1 - parity)}
        route = [pair for pair in matching(groups, 1, parity) if pair[0] in holders]
        arrays = (lax.ppermute(near[1 - parity][0], "frame", route), lax.ppermute(near[1 - parity][1], "frame", route))
        far_blocks.append(("pair", ("relay", 2, parity), arrays))

    for level in range(2, levels):
        for parity in (0, 1):
            route = matching(groups, 2**level, parity)
            if route:
                arrays = tuple(lax.ppermute(array, "frame", route) for array in (keys, values))
                far_blocks.append(("pair", ("frame", 2**level, parity), arrays))

    stacked, query_copy, tables = fetch(tables, queries, keys, values)
    state, query_parts = attend_own(query_copy, stacked)

    half = blocks // 2
    half_blocks = []
    early_blocks = []
    side_blocks = []
    for distance in range(half, 0, -1):
        for parity in (0, 1):
            route = matching(blocks, distance, parity)
            if not route:
                continue
            which = ("space", distance, parity)
            if distance == half:
                halved = lax.ppermute(stacked, "space", route)
                half_blocks.append(("stacked", which, (halved,)))
                continue
            source = stacked
            nearer = through_half(route, blocks) if parity else None
            if nearer:
                route, source = nearer, halved
            array = lax.ppermute(source, "space", route)
            (side_blocks if parity else early_blocks).append(("stacked", which, (array,)))

    single = len(far_blocks) == 2 and groups <= 2 * far_distance
    final = far_blocks if single else (near_blocks + far_blocks)[-1:]
    near_blocks, far_blocks = (
        [block for block in group if all(block is not other for other in final)]
        for group in (near_blocks, far_blocks)
    )
    state = attend_all(state, tables, query_parts, near_blocks + early_blocks)
    state = attend_all(state, tables, query_parts, half_blocks)
    state = attend_all(state, tables, query_parts, side_blocks[1:] + far_blocks)
    return finish(state, tables, query_parts, side_blocks[:1], final)


def solution(mesh):
    rows = P(("groups", "frame", "space"), None)
    return jax.shard_map(attention, mesh=mesh, in_specs=(rows, rows, rows, P(), P()), out_specs=rows, check_vma=False)
```

time: 45 us -> 41.8 us (0.929)
  the two profiles are of different devices: /device:TPU:0 before, /device:TPU:2 now
where the time goes in v3:
time: 41.8 us; the launch traced here: 41.5 us
  waiting for transfers between devices  23.2 us (56%)
  Pallas kernels  9.38 us (22%)
  starting transfers between devices  8.8 us (21%)
    ppermute x1, waiting for transfers between devices, attention(): halved = lax.ppermute(stacked, 'space', route)  10.8 us
    ppermute x2, waiting for transfers between devices, attention(): lax.ppermute(near[1 - parity][1], 'frame', route)  6.39 us
    ppermute x2, waiting for transfers between devices, attention(): lax.ppermute(near[1 - parity][0], 'frame', route)  5.96 us
    pallas_call x2, Pallas kernels, attend(): pl.pallas_call(functools.partial(attend_kernel, plan), in_specs=[whole] *...  3.96 us
    ppermute x2, starting transfers between devices, attention(): lax.ppermute(values, 'frame', route)  2.77 us
    ppermute x2, starting transfers between devices, attention(): lax.ppermute(near[1 - parity][0], 'frame', route)  1.97 us
    ppermute x2, starting transfers between devices, attention(): lax.ppermute(near[1 - parity][1], 'frame', route)  1.97 us
    pallas_call x1, Pallas kernels, finish(): pl.pallas_call(functools.partial(weigh_kernel, plan, whiches), in_specs=[...  1.72 us
  transfers between devices with their start and end apart: 11, of which 3 were waited for; matrix products, arithmetic and copies ran while one was open for 0% of the time, Pallas kernels for 16%

profile of v3, /device:TPU:2, one launch (start us, length us, event | category | flops | bytes accessed | tf_op | source)
XLA Modules:
  0.0 41.5 jit_solution(14757090912380945824)
XLA Ops:
  0.0 0.0 copy-start.1
  0.0 0.0 copy-start
  0.0 1.3 %shard_map.55 = (f32[1024,128]{1,0:T(8,128)S(1)}, f32[512,128]{1,0:T(8,128)S(1)}, s32[4,4]{1,0:T(4,128)S(1)}, s32[2,2,4]{2,1,0:T(2,128)S(1)}) custom-call(s32[4,4]{1,0:T(4,128)} %block_mask.1, s32[2,2,4]{2,1,0:T(2,128)} %bitcast.1, f32[512,128]{1,0:T(8,128)} %queries.1, f32[512,128]{1,0:T(8,128)} %keys.1, f32[512,128]{1,0:T(8,128)} %values.1), custom_call_target="tpu_custom_call" | custom-call | tf_op jit(solution)/shard_map/pallas_call | solution.py:256
  1.3 0.1 collective-permute-start.4
  1.4 0.0 copy-done.1
  1.4 2.1 %collective-permute-start = (f32[512,128]{1,0:T(8,128)S(1)}, f32[512,128]{1,0:T(8,128)S(1)}, u32[]{:S(2)}, u32[]{:S(2)}) collective-permute-start(f32[512,128]{1,0:T(8,128)S(1)} %copy-done.1), channel_id=1, source_target_pairs={{0,4},{8,12},{4,0},{12,8},{1,5},{9,13},{5,1},{13,9},{2,6},{10,14},... | collective-permute-start | bytes 786440 | tf_op jit(solution)/shard_map/ppermute | solution.py:372
  3.5 0.0 collective-permute-start.10
  3.5 0.0 copy-done
  3.5 0.1 collective-permute-start.6
  3.6 0.7 %collective-permute-start.8 = (f32[512,128]{1,0:T(8,128)S(1)}, f32[512,128]{1,0:T(8,128)S(1)}, u32[]{:S(2)}, u32[]{:S(2)}) collective-permute-start(f32[512,128]{1,0:T(8,128)S(1)} %copy-done), channel_id=1, source_target_pairs={{4,8},{8,4},{5,9},{9,5},{6,10},{10,6},{7,11},{11,7},{20,24},{24,20... | collective-permute-start | bytes 786440 | tf_op jit(solution)/shard_map/ppermute | solution.py:372
  4.3 10.8 %collective-permute-done.4.refs_0_ = f32[1024,128]{1,0:T(8,128)S(1)} collective-permute-done((f32[1024,128]{1,0:T(8,128)S(1)}, f32[1024,128]{1,0:T(8,128)S(1)}, u32[]{:S(2)}, u32[]{:S(2)}) %collective-permute-start.4) | collective-permute-done | bytes 524320 | tf_op jit(solution)/shard_map/ppermute | solution.py:403
  15.1 1.3 %collective-permute-start.5 = (f32[1024,128]{1,0:T(8,128)S(1)}, f32[1024,128]{1,0:T(8,128)S(1)}, u32[]{:S(2)}, u32[]{:S(2)}) collective-permute-start(f32[1024,128]{1,0:T(8,128)S(1)} %collective-permute-done.4.refs_0_), channel_id=1, source_target_pairs={{3,2},{0,1},{7,6},{4,5},{11,10},{8,9},{15,14},{12,13},{19,18},{16,... | collective-permute-start | bytes 1572872 | tf_op jit(solution)/shard_map/ppermute | solution.py:410
  16.4 0.0 collective-permute-done.refs_3_
  16.4 0.7 %collective-permute-start.2 = (f32[512,128]{1,0:T(8,128)S(1)}, f32[512,128]{1,0:T(8,128)S(1)}, u32[]{:S(2)}, u32[]{:S(2)}) collective-permute-start(f32[512,128]{1,0:T(8,128)S(1)} %copy-done.1), channel_id=1, source_target_pairs={{4,8},{8,4},{5,9},{9,5},{6,10},{10,6},{7,11},{11,7},{20,24},{24,20... | collective-permute-start | bytes 786440 | tf_op jit(solution)/shard_map/ppermute | solution.py:372
  17.1 0.0 collective-permute-done.6.refs_2_
  17.1 0.7 %collective-permute-start.7 = (f32[512,128]{1,0:T(8,128)S(1)}, f32[512,128]{1,0:T(8,128)S(1)}, u32[]{:S(2)}, u32[]{:S(2)}) collective-permute-start(f32[512,128]{1,0:T(8,128)S(1)} %collective-permute-done.6.refs_2_), channel_id=1, source_target_pairs={{4,8},{8,4},{5,9},{9,5},{6,10},{10,6},{7,11},{11,7},{20,24},{24,20... | collective-permute-start | bytes 786440 | tf_op jit(solution)/shard_map/ppermute | solution.py:379
  17.8 0.0 collective-permute-done.8.refs_0_
  17.8 1.3 %collective-permute-start.9 = (f32[512,128]{1,0:T(8,128)S(1)}, f32[512,128]{1,0:T(8,128)S(1)}, u32[]{:S(2)}, u32[]{:S(2)}) collective-permute-start(f32[512,128]{1,0:T(8,128)S(1)} %collective-permute-done.8.refs_0_), channel_id=1, source_target_pairs={{8,12},{4,0},{9,13},{5,1},{10,14},{6,2},{11,15},{7,3},{24,28},{20,... | collective-permute-start | bytes 786440 | tf_op jit(solution)/shard_map/ppermute | solution.py:379
  19.1 1.1 %shard_map.56 = (f32[512,128]{1,0:T(8,128)S(1)}, f32[512,128]{1,0:T(8,128)S(1)}, f32[512,256]{1,0:T(8,128)S(1)}, bf16[512,512]{1,0:T(8,128)(2,1)S(1)}) custom-call(f32[512,128]{1,0:T(8,128)S(1)} %get-tuple-element.25.queries, f32[1024,128]{1,0:T(8,128)S(1)} %get-tuple-element.26.stacked), custom_call_target="tpu_custom_call" | custom-call | flops 536870912 | bytes 524288 | tf_op jit(solution)/shard_map/pallas_call | solution.py:270
  20.2 0.0 collective-permute-done.2.refs_1_
  20.2 0.7 %collective-permute-start.1 = (f32[512,128]{1,0:T(8,128)S(1)}, f32[512,128]{1,0:T(8,128)S(1)}, u32[]{:S(2)}, u32[]{:S(2)}) collective-permute-start(f32[512,128]{1,0:T(8,128)S(1)} %collective-permute-done.refs_3_), channel_id=1, source_target_pairs={{4,8},{8,4},{5,9},{9,5},{6,10},{10,6},{7,11},{11,7},{20,24},{24,20... | collective-permute-start | bytes 786440 | tf_op jit(solution)/shard_map/ppermute | solution.py:379
  20.9 0.0 collective-permute-done.10.refs_4_
  20.9 1.3 %collective-permute-start.3 = (f32[512,128]{1,0:T(8,128)S(1)}, f32[512,128]{1,0:T(8,128)S(1)}, u32[]{:S(2)}, u32[]{:S(2)}) collective-permute-start(f32[512,128]{1,0:T(8,128)S(1)} %collective-permute-done.2.refs_1_), channel_id=1, source_target_pairs={{8,12},{4,0},{9,13},{5,1},{10,14},{6,2},{11,15},{7,3},{24,28},{20,... | collective-permute-start | bytes 786440 | tf_op jit(solution)/shard_map/ppermute | solution.py:379
  22.2 2.6 %shard_map.57 = (f32[512,128]{1,0:T(8,128)S(1)}, f32[512,128]{1,0:T(8,128)S(1)}, f32[512,256]{1,0:T(8,128)S(1)}) custom-call(s32[4,4]{1,0:T(4,128)S(1)} %get-tuple-element.23.block_mask, s32[2,2,4]{2,1,0:T(2,128)S(1)} %get-tuple-element.24.partner_flags, bf16[512,512]{1,0:T(8,128)(2,1)S(1)} %get-tuple-element.27.query_parts, ...), custom_call_target="tpu_custom_call" | custom-call | flops 1610612736 | bytes 1572864 | tf_op jit(solution)/shard_map/pallas_call | solution.py:291
  24.8 1.3 %shard_map.58 = (f32[512,128]{1,0:T(8,128)S(1)}, f32[512,128]{1,0:T(8,128)S(1)}, f32[512,256]{1,0:T(8,128)S(1)}) custom-call(s32[4,4]{1,0:T(4,128)S(1)} %get-tuple-element.23.block_mask, s32[2,2,4]{2,1,0:T(2,128)S(1)} %get-tuple-element.24.partner_flags, bf16[512,512]{1,0:T(8,128)(2,1)S(1)} %get-tuple-element.27.query_parts, ...), custom_call_target="tpu_custom_call" | custom-call | flops 536870912 | bytes 524288 | tf_op jit(solution)/shard_map/pallas_call | solution.py:291
  26.2 0.0 collective-permute-done.7.refs_1_
  26.2 6.0 %collective-permute-done.9.refs_2_ = f32[512,128]{1,0:T(8,128)S(1)} collective-permute-done((f32[512,128]{1,0:T(8,128)S(1)}, f32[512,128]{1,0:T(8,128)S(1)}, u32[]{:S(2)}, u32[]{:S(2)}) %collective-permute-start.9) | collective-permute-done | bytes 262176 | tf_op jit(solution)/shard_map/ppermute | solution.py:379
  32.2 0.0 collective-permute-done.5.refs_0_
  32.2 1.7 %shard_map.59 = (bf16[512,512]{1,0:T(8,128)(2,1)S(1)}, bf16[512,512]{1,0:T(8,128)(2,1)S(1)}, f32[512,128]{1,0:T(8,128)S(1)}, f32[512,128]{1,0:T(8,128)S(1)}) custom-call(s32[4,4]{1,0:T(4,128)S(1)} %get-tuple-element.23.block_mask, s32[2,2,4]{2,1,0:T(2,128)S(1)} %get-tuple-element.24.partner_flags, bf16[512,512]{1,0:T(8,128)(2,1)S(1)} %get-tuple-element.27.query_parts, ...), custom_call_target="tpu_custom_call" | custom-call | flops 1073741824 | bytes 1048576 | tf_op jit(solution)/shard_map/pallas_call | solution.py:312
  33.9 0.0 collective-permute-done.1.refs_0_
  33.9 6.4 %collective-permute-done.3.refs_1_ = f32[512,128]{1,0:T(8,128)S(1)} collective-permute-done((f32[512,128]{1,0:T(8,128)S(1)}, f32[512,128]{1,0:T(8,128)S(1)}, u32[]{:S(2)}, u32[]{:S(2)}) %collective-permute-start.3) | collective-permute-done | bytes 262176 | tf_op jit(solution)/shard_map/ppermute | solution.py:379
  40.3 1.2 %shard_map.60 = f32[512,128]{1,0:T(8,128)} custom-call(s32[4,4]{1,0:T(4,128)S(1)} %get-tuple-element.23.block_mask, s32[2,2,4]{2,1,0:T(2,128)S(1)} %get-tuple-element.24.partner_flags, f32[512,128]{1,0:T(8,128)S(1)} %collective-permute-done.1.refs_0_, f32[512,128]{1,0:T(8,128)S(1)} %collective-permute-done.3.refs_1_, ...), custom_call_target="tpu_custom_call" | custom-call | flops 536870912 | bytes 524288 | tf_op jit(solution)/shard_map/pallas_call | solution.py:326
Async XLA Ops:
  0.0 1.4 %copy-start.1 = (f32[512,128]{1,0:T(8,128)S(1)}, f32[512,128]{1,0:T(8,128)}, u32[]{:S(2)}) copy-start(f32[512,128]{1,0:T(8,128)} %values.1) | copy-start | bytes 786436
  0.0 3.5 %copy-start = (f32[512,128]{1,0:T(8,128)S(1)}, f32[512,128]{1,0:T(8,128)}, u32[]{:S(2)}) copy-start(f32[512,128]{1,0:T(8,128)} %keys.1) | copy-start | bytes 786436
  1.3 13.7 %collective-permute-start.4 = (f32[1024,128]{1,0:T(8,128)S(1)}, f32[1024,128]{1,0:T(8,128)S(1)}, u32[]{:S(2)}, u32[]{:S(2)}) collective-permute-start(f32[1024,128]{1,0:T(8,128)S(1)} %get-tuple-element.26.stacked), channel_id=1, source_target_pairs={{0,2},{1,3},{2,0},{3,1},{4,6},{5,7},{6,4},{7,5},{8,10},{9,11},{10,... | collective-permute-start | bytes 1572872 | tf_op jit(solution)/shard_map/ppermute | solution.py:403
  1.4 14.9 %collective-permute-start = (f32[512,128]{1,0:T(8,128)S(1)}, f32[512,128]{1,0:T(8,128)S(1)}, u32[]{:S(2)}, u32[]{:S(2)}) collective-permute-start(f32[512,128]{1,0:T(8,128)S(1)} %copy-done.1), channel_id=1, source_target_pairs={{0,4},{8,12},{4,0},{12,8},{1,5},{9,13},{5,1},{13,9},{2,6},{10,14},... | collective-permute-start | bytes 786440 | tf_op jit(solution)/shard_map/ppermute | solution.py:372
  3.5 17.4 %collective-permute-start.10 = (f32[1024,128]{1,0:T(8,128)S(1)}, f32[1024,128]{1,0:T(8,128)S(1)}, u32[]{:S(2)}, u32[]{:S(2)}) collective-permute-start(f32[1024,128]{1,0:T(8,128)S(1)} %get-tuple-element.26.stacked), channel_id=1, source_target_pairs={{0,1},{2,3},{1,0},{3,2},{4,5},{6,7},{5,4},{7,6},{8,9},{10,11},{9,8... | collective-permute-start | bytes 1572872 | tf_op jit(solution)/shard_map/ppermute | solution.py:410
  3.5 13.5 %collective-permute-start.6 = (f32[512,128]{1,0:T(8,128)S(1)}, f32[512,128]{1,0:T(8,128)S(1)}, u32[]{:S(2)}, u32[]{:S(2)}) collective-permute-start(f32[512,128]{1,0:T(8,128)S(1)} %copy-done), channel_id=1, source_target_pairs={{0,4},{8,12},{4,0},{12,8},{1,5},{9,13},{5,1},{13,9},{2,6},{10,14},... | collective-permute-start | bytes 786440 | tf_op jit(solution)/shard_map/ppermute | solution.py:372
  3.6 14.1 %collective-permute-start.8 = (f32[512,128]{1,0:T(8,128)S(1)}, f32[512,128]{1,0:T(8,128)S(1)}, u32[]{:S(2)}, u32[]{:S(2)}) collective-permute-start(f32[512,128]{1,0:T(8,128)S(1)} %copy-done), channel_id=1, source_target_pairs={{4,8},{8,4},{5,9},{9,5},{6,10},{10,6},{7,11},{11,7},{20,24},{24,20... | collective-permute-start | bytes 786440 | tf_op jit(solution)/shard_map/ppermute | solution.py:372
  15.1 17.1 %collective-permute-start.5 = (f32[1024,128]{1,0:T(8,128)S(1)}, f32[1024,128]{1,0:T(8,128)S(1)}, u32[]{:S(2)}, u32[]{:S(2)}) collective-permute-start(f32[1024,128]{1,0:T(8,128)S(1)} %collective-permute-done.4.refs_0_), channel_id=1, source_target_pairs={{3,2},{0,1},{7,6},{4,5},{11,10},{8,9},{15,14},{12,13},{19,18},{16,... | collective-permute-start | bytes 1572872 | tf_op jit(solution)/shard_map/ppermute | solution.py:410
  16.4 3.8 %collective-permute-start.2 = (f32[512,128]{1,0:T(8,128)S(1)}, f32[512,128]{1,0:T(8,128)S(1)}, u32[]{:S(2)}, u32[]{:S(2)}) collective-permute-start(f32[512,128]{1,0:T(8,128)S(1)} %copy-done.1), channel_id=1, source_target_pairs={{4,8},{8,4},{5,9},{9,5},{6,10},{10,6},{7,11},{11,7},{20,24},{24,20... | collective-permute-start | bytes 786440 | tf_op jit(solution)/shard_map/ppermute | solution.py:372
  17.1 9.1 %collective-permute-start.7 = (f32[512,128]{1,0:T(8,128)S(1)}, f32[512,128]{1,0:T(8,128)S(1)}, u32[]{:S(2)}, u32[]{:S(2)}) collective-permute-start(f32[512,128]{1,0:T(8,128)S(1)} %collective-permute-done.6.refs_2_), channel_id=1, source_target_pairs={{4,8},{8,4},{5,9},{9,5},{6,10},{10,6},{7,11},{11,7},{20,24},{24,20... | collective-permute-start | bytes 786440 | tf_op jit(solution)/shard_map/ppermute | solution.py:379
  17.8 14.4 %collective-permute-start.9 = (f32[512,128]{1,0:T(8,128)S(1)}, f32[512,128]{1,0:T(8,128)S(1)}, u32[]{:S(2)}, u32[]{:S(2)}) collective-permute-start(f32[512,128]{1,0:T(8,128)S(1)} %collective-permute-done.8.refs_0_), channel_id=1, source_target_pairs={{8,12},{4,0},{9,13},{5,1},{10,14},{6,2},{11,15},{7,3},{24,28},{20,... | collective-permute-start | bytes 786440 | tf_op jit(solution)/shard_map/ppermute | solution.py:379
  20.2 13.7 %collective-permute-start.1 = (f32[512,128]{1,0:T(8,128)S(1)}, f32[512,128]{1,0:T(8,128)S(1)}, u32[]{:S(2)}, u32[]{:S(2)}) collective-permute-start(f32[512,128]{1,0:T(8,128)S(1)} %collective-permute-done.refs_3_), channel_id=1, source_target_pairs={{4,8},{8,4},{5,9},{9,5},{6,10},{10,6},{7,11},{11,7},{20,24},{24,20... | collective-permute-start | bytes 786440 | tf_op jit(solution)/shard_map/ppermute | solution.py:379
  20.9 19.4 %collective-permute-start.3 = (f32[512,128]{1,0:T(8,128)S(1)}, f32[512,128]{1,0:T(8,128)S(1)}, u32[]{:S(2)}, u32[]{:S(2)}) collective-permute-start(f32[512,128]{1,0:T(8,128)S(1)} %collective-permute-done.2.refs_1_), channel_id=1, source_target_pairs={{8,12},{4,0},{9,13},{5,1},{10,14},{6,2},{11,15},{7,3},{24,28},{20,... | collective-permute-start | bytes 786440 | tf_op jit(solution)/shard_map/ppermute | solution.py:379

commit v4 on v3

--- a/solution.py
+++ b/solution.py
@@ -348,6 +348,21 @@
     return [(i, i + distance) for i in lower] + [(i + distance, i) for i in lower]
 
 
+def both_ways(route):
+    sources = {source for source, _ in route}
+    targets = {target for _, target in route}
+    return route + [(two, one) for one, two in route if two not in sources and one not in targets]
+
+
+def moved_along_frames(array, route):
+    blocks = lax.axis_size("space")
+    left_out = set(range(lax.axis_size("frame"))) - {frame for pair in route for frame in pair}
+    pairs = [(one * blocks + s, two * blocks + s) for one, two in route for s in range(blocks)]
+    for frame in sorted(left_out):
+        pairs += [(frame * blocks + one, frame * blocks + two) for one, two in matching(blocks, 1, 0)]
+    return lax.ppermute(array, ("frame", "space"), pairs)
+
+
 def through_half(route, size):
     half = size // 2
     pairs = []
@@ -369,14 +384,14 @@
     for parity in (1, 0):
         route = matching(groups, 1, parity)
         if route:
-            near[parity] = (lax.ppermute(keys, "frame", route), lax.ppermute(values, "frame", route))
+            near[parity] = (moved_along_frames(keys, route), moved_along_frames(values, route))
     near_blocks = [("pair", ("frame", 1, parity), arrays) for parity, arrays in near.items()]
 
     far_blocks = []
     for parity in (1, 0) if levels > 1 and len(near) == 2 else ():
         holders = {target for _, target in matching(groups, 1, 1 - parity)}
         route = [pair for pair in matching(groups, 1, parity) if pair[0] in holders]
-        arrays = (lax.ppermute(near[1 - parity][0], "frame", route), lax.ppermute(near[1 - parity][1], "frame", route))
+        arrays = (moved_along_frames(near[1 - parity][0], route), moved_along_frames(near[1 - parity][1], route))
         far_blocks.append(("pair", ("relay", 2, parity), arrays))
 
     for level in range(2, levels):
@@ -406,7 +421,7 @@
             source = stacked
             nearer = through_half(route, blocks) if parity else None
             if nearer:
-                route, source = nearer, halved
+                route, source = both_ways(nearer), halved
             array = lax.ppermute(source, "space", route)
             (side_blocks if parity else early_blocks).append(("stacked", which, (array,)))
 
@@ -416,8 +431,7 @@
         [block for block in group if all(block is not other for other in final)]
         for group in (near_blocks, far_blocks)
     )
-    state = attend_all(state, tables, query_parts, near_blocks + early_blocks)
-    state = attend_all(state, tables, query_parts, half_blocks)
+    state = attend_all(state, tables, query_parts, near_blocks + early_blocks + half_blocks)
     state = attend_all(state, tables, query_parts, side_blocks[1:] + far_blocks)
     return finish(state, tables, query_parts, side_blocks[:1], final)
 

time: 41.8 us -> 36.9 us (0.88)
  the two profiles are of different devices: /device:TPU:2 before, /device:TPU:0 now
where the time goes in v4:
time: 36.9 us; the launch traced here: 36.8 us
  waiting for transfers between devices  19.1 us (52%)
  starting transfers between devices  8.94 us (24%)
  Pallas kernels  8.6 us (23%)
    ppermute x1, waiting for transfers between devices, attention(): halved = lax.ppermute(stacked, 'space', route)  9.66 us
    ppermute x8, waiting for transfers between devices, moved_along_frames(): return lax.ppermute(array, ('frame', 'space'), pairs)  9.48 us
    ppermute x8, starting transfers between devices, moved_along_frames(): return lax.ppermute(array, ('frame', 'space'), pairs)  5.9 us
    pallas_call x1, Pallas kernels, attend(): pl.pallas_call(functools.partial(attend_kernel, plan), in_specs=[whole] *...  3.2 us
    ppermute x1, starting transfers between devices, attention(): halved = lax.ppermute(stacked, 'space', route)  3.03 us
    pallas_call x1, Pallas kernels, finish(): pl.pallas_call(functools.partial(weigh_kernel, plan, whiches), in_specs=[...  1.7 us
    pallas_call x1, Pallas kernels, fetch(): pl.pallas_call(fetch_kernel, in_specs=[pl.BlockSpec(memory_space=pltpu.HB...  1.33 us
    pallas_call x1, Pallas kernels, finish(): pl.pallas_call(functools.partial(finish_kernel, whiches), in_specs=[whole...  1.22 us
  transfers between devices with their start and end apart: 11, of which 4 were waited for; matrix products, arithmetic and copies ran while one was open for 0% of the time, Pallas kernels for 16%

profile of v4, /device:TPU:0, one launch (start us, length us, event | category | flops | bytes accessed | tf_op | source)
XLA Modules:
  0.0 36.8 jit_solution(14444916737560022317)
XLA Ops:
  0.0 0.0 copy-start.1
  0.0 0.0 copy-start
  0.0 1.3 %shard_map.55 = (f32[1024,128]{1,0:T(8,128)S(1)}, f32[512,128]{1,0:T(8,128)S(1)}, s32[4,4]{1,0:T(4,128)S(1)}, s32[2,2,4]{2,1,0:T(2,128)S(1)}) custom-call(s32[4,4]{1,0:T(4,128)} %block_mask.1, s32[2,2,4]{2,1,0:T(2,128)} %bitcast.1, f32[512,128]{1,0:T(8,128)} %queries.1, f32[512,128]{1,0:T(8,128)} %keys.1, f32[512,128]{1,0:T(8,128)} %values.1), custom_call_target="tpu_custom_call" | custom-call | tf_op jit(solution)/shard_map/pallas_call | solution.py:256
  1.3 3.0 %collective-permute-start.4 = (f32[1024,128]{1,0:T(8,128)S(1)}, f32[1024,128]{1,0:T(8,128)S(1)}, u32[]{:S(2)}, u32[]{:S(2)}) collective-permute-start(f32[1024,128]{1,0:T(8,128)S(1)} %get-tuple-element.23.stacked), channel_id=1, source_target_pairs={{0,2},{1,3},{2,0},{3,1},{4,6},{5,7},{6,4},{7,5},{8,10},{9,11},{10,... | collective-permute-start | bytes 1572872 | tf_op jit(solution)/shard_map/ppermute | solution.py:418
  4.4 0.0 copy-done.1
  4.4 1.6 %collective-permute-start = (f32[512,128]{1,0:T(8,128)S(1)}, f32[512,128]{1,0:T(8,128)S(1)}, u32[]{:S(2)}, u32[]{:S(2)}) collective-permute-start(f32[512,128]{1,0:T(8,128)S(1)} %copy-done.1), channel_id=1, source_target_pairs={{0,4},{1,5},{2,6},{3,7},{8,12},{9,13},{10,14},{11,15},{4,0},{5,1},... | collective-permute-start | bytes 786440 | tf_op jit(solution)/shard_map/ppermute | solution.py:363
  6.0 0.0 collective-permute-start.10
  6.0 0.0 copy-done
  6.0 0.5 %collective-permute-start.6 = (f32[512,128]{1,0:T(8,128)S(1)}, f32[512,128]{1,0:T(8,128)S(1)}, u32[]{:S(2)}, u32[]{:S(2)}) collective-permute-start(f32[512,128]{1,0:T(8,128)S(1)} %copy-done), channel_id=1, source_target_pairs={{0,4},{1,5},{2,6},{3,7},{8,12},{9,13},{10,14},{11,15},{4,0},{5,1},... | collective-permute-start | bytes 786440 | tf_op jit(solution)/shard_map/ppermute | solution.py:363
  6.4 0.2 collective-permute-start.8
  6.6 9.7 %collective-permute-done.4.refs_5_ = f32[1024,128]{1,0:T(8,128)S(1)} collective-permute-done((f32[1024,128]{1,0:T(8,128)S(1)}, f32[1024,128]{1,0:T(8,128)S(1)}, u32[]{:S(2)}, u32[]{:S(2)}) %collective-permute-start.4) | collective-permute-done | bytes 524320 | tf_op jit(solution)/shard_map/ppermute | solution.py:418
  16.3 0.0 collective-permute-start.5
  16.3 0.0 collective-permute-done.refs_3_
  16.3 0.5 %collective-permute-start.2 = (f32[512,128]{1,0:T(8,128)S(1)}, f32[512,128]{1,0:T(8,128)S(1)}, u32[]{:S(2)}, u32[]{:S(2)}) collective-permute-start(f32[512,128]{1,0:T(8,128)S(1)} %copy-done.1), channel_id=1, source_target_pairs={{4,8},{5,9},{6,10},{7,11},{8,4},{9,5},{10,6},{11,7},{0,1},{2,3},{1... | collective-permute-start | bytes 786440 | tf_op jit(solution)/shard_map/ppermute | solution.py:363
  16.8 0.9 %collective-permute-done.6.refs_2_ = f32[512,128]{1,0:T(8,128)S(1)} collective-permute-done((f32[512,128]{1,0:T(8,128)S(1)}, f32[512,128]{1,0:T(8,128)S(1)}, u32[]{:S(2)}, u32[]{:S(2)}) %collective-permute-start.6) | collective-permute-done | bytes 262176 | tf_op jit(solution)/shard_map/ppermute | solution.py:363
  17.8 0.0 collective-permute-start.7
  17.8 0.0 collective-permute-done.8.refs_0_
  17.8 1.3 %collective-permute-start.9 = (f32[512,128]{1,0:T(8,128)S(1)}, f32[512,128]{1,0:T(8,128)S(1)}, u32[]{:S(2)}, u32[]{:S(2)}) collective-permute-start(f32[512,128]{1,0:T(8,128)S(1)} %collective-permute-done.8.refs_0_), channel_id=1, source_target_pairs={{8,12},{9,13},{10,14},{11,15},{4,0},{5,1},{6,2},{7,3},{24,28},{25,... | collective-permute-start | bytes 786440 | tf_op jit(solution)/shard_map/ppermute | solution.py:363
  19.1 1.1 %shard_map.56 = (f32[512,128]{1,0:T(8,128)S(1)}, f32[512,128]{1,0:T(8,128)S(1)}, f32[512,256]{1,0:T(8,128)S(1)}, bf16[512,512]{1,0:T(8,128)(2,1)S(1)}) custom-call(f32[512,128]{1,0:T(8,128)S(1)} %get-tuple-element.22.queries, f32[1024,128]{1,0:T(8,128)S(1)} %get-tuple-element.23.stacked), custom_call_target="tpu_custom_call" | custom-call | flops 536870912 | bytes 524288 | tf_op jit(solution)/shard_map/pallas_call | solution.py:270
  20.2 0.0 collective-permute-done.2.refs_1_
  20.2 0.6 %collective-permute-start.1 = (f32[512,128]{1,0:T(8,128)S(1)}, f32[512,128]{1,0:T(8,128)S(1)}, u32[]{:S(2)}, u32[]{:S(2)}) collective-permute-start(f32[512,128]{1,0:T(8,128)S(1)} %collective-permute-done.refs_3_), channel_id=1, source_target_pairs={{4,8},{5,9},{6,10},{7,11},{8,4},{9,5},{10,6},{11,7},{0,1},{2,3},{1... | collective-permute-start | bytes 786440 | tf_op jit(solution)/shard_map/ppermute | solution.py:363
  20.8 0.0 collective-permute-done.10.refs_4_
  20.8 1.3 %collective-permute-start.3 = (f32[512,128]{1,0:T(8,128)S(1)}, f32[512,128]{1,0:T(8,128)S(1)}, u32[]{:S(2)}, u32[]{:S(2)}) collective-permute-start(f32[512,128]{1,0:T(8,128)S(1)} %collective-permute-done.2.refs_1_), channel_id=1, source_target_pairs={{8,12},{9,13},{10,14},{11,15},{4,0},{5,1},{6,2},{7,3},{24,28},{25,... | collective-permute-start | bytes 786440 | tf_op jit(solution)/shard_map/ppermute | solution.py:363
  22.1 3.2 %shard_map.57 = (f32[512,128]{1,0:T(8,128)S(1)}, f32[512,128]{1,0:T(8,128)S(1)}, f32[512,256]{1,0:T(8,128)S(1)}) custom-call(s32[4,4]{1,0:T(4,128)S(1)} %get-tuple-element.20.block_mask, s32[2,2,4]{2,1,0:T(2,128)S(1)} %get-tuple-element.21.partner_flags, bf16[512,512]{1,0:T(8,128)(2,1)S(1)} %get-tuple-element.24.query_parts, ...), custom_call_target="tpu_custom_call" | custom-call | flops 2147483648 | bytes 2097152 | tf_op jit(solution)/shard_map/pallas_call | solution.py:291
  25.3 0.0 collective-permute-done.7.refs_1_
  25.3 3.1 %collective-permute-done.9.refs_2_ = f32[512,128]{1,0:T(8,128)S(1)} collective-permute-done((f32[512,128]{1,0:T(8,128)S(1)}, f32[512,128]{1,0:T(8,128)S(1)}, u32[]{:S(2)}, u32[]{:S(2)}) %collective-permute-start.9) | collective-permute-done | bytes 262176 | tf_op jit(solution)/shard_map/ppermute | solution.py:363
  28.4 0.0 collective-permute-done.5.refs_0_
  28.4 1.7 %shard_map.58 = (bf16[512,512]{1,0:T(8,128)(2,1)S(1)}, bf16[512,512]{1,0:T(8,128)(2,1)S(1)}, f32[512,128]{1,0:T(8,128)S(1)}, f32[512,128]{1,0:T(8,128)S(1)}) custom-call(s32[4,4]{1,0:T(4,128)S(1)} %get-tuple-element.20.block_mask, s32[2,2,4]{2,1,0:T(2,128)S(1)} %get-tuple-element.21.partner_flags, bf16[512,512]{1,0:T(8,128)(2,1)S(1)} %get-tuple-element.24.query_parts, ...), custom_call_target="tpu_custom_call" | custom-call | flops 1073741824 | bytes 1048576 | tf_op jit(solution)/shard_map/pallas_call | solution.py:312
  30.1 0.0 collective-permute-done.1.refs_0_
  30.1 5.5 %collective-permute-done.3.refs_1_ = f32[512,128]{1,0:T(8,128)S(1)} collective-permute-done((f32[512,128]{1,0:T(8,128)S(1)}, f32[512,128]{1,0:T(8,128)S(1)}, u32[]{:S(2)}, u32[]{:S(2)}) %collective-permute-start.3) | collective-permute-done | bytes 262176 | tf_op jit(solution)/shard_map/ppermute | solution.py:363
  35.5 1.2 %shard_map.59 = f32[512,128]{1,0:T(8,128)} custom-call(s32[4,4]{1,0:T(4,128)S(1)} %get-tuple-element.20.block_mask, s32[2,2,4]{2,1,0:T(2,128)S(1)} %get-tuple-element.21.partner_flags, f32[512,128]{1,0:T(8,128)S(1)} %collective-permute-done.1.refs_0_, f32[512,128]{1,0:T(8,128)S(1)} %collective-permute-done.3.refs_1_, ...), custom_call_target="tpu_custom_call" | custom-call | flops 536870912 | bytes 524288 | tf_op jit(solution)/shard_map/pallas_call | solution.py:326
Async XLA Ops:
  0.0 4.4 %copy-start.1 = (f32[512,128]{1,0:T(8,128)S(1)}, f32[512,128]{1,0:T(8,128)}, u32[]{:S(2)}) copy-start(f32[512,128]{1,0:T(8,128)} %values.1) | copy-start | bytes 786436
  0.0 6.0 %copy-start = (f32[512,128]{1,0:T(8,128)S(1)}, f32[512,128]{1,0:T(8,128)}, u32[]{:S(2)}) copy-start(f32[512,128]{1,0:T(8,128)} %keys.1) | copy-start | bytes 786436
  1.3 15.0 %collective-permute-start.4 = (f32[1024,128]{1,0:T(8,128)S(1)}, f32[1024,128]{1,0:T(8,128)S(1)}, u32[]{:S(2)}, u32[]{:S(2)}) collective-permute-start(f32[1024,128]{1,0:T(8,128)S(1)} %get-tuple-element.23.stacked), channel_id=1, source_target_pairs={{0,2},{1,3},{2,0},{3,1},{4,6},{5,7},{6,4},{7,5},{8,10},{9,11},{10,... | collective-permute-start | bytes 1572872 | tf_op jit(solution)/shard_map/ppermute | solution.py:418
  4.4 11.9 %collective-permute-start = (f32[512,128]{1,0:T(8,128)S(1)}, f32[512,128]{1,0:T(8,128)S(1)}, u32[]{:S(2)}, u32[]{:S(2)}) collective-permute-start(f32[512,128]{1,0:T(8,128)S(1)} %copy-done.1), channel_id=1, source_target_pairs={{0,4},{1,5},{2,6},{3,7},{8,12},{9,13},{10,14},{11,15},{4,0},{5,1},... | collective-permute-start | bytes 786440 | tf_op jit(solution)/shard_map/ppermute | solution.py:363
  6.0 14.8 %collective-permute-start.10 = (f32[1024,128]{1,0:T(8,128)S(1)}, f32[1024,128]{1,0:T(8,128)S(1)}, u32[]{:S(2)}, u32[]{:S(2)}) collective-permute-start(f32[1024,128]{1,0:T(8,128)S(1)} %get-tuple-element.23.stacked), channel_id=1, source_target_pairs={{0,1},{2,3},{1,0},{3,2},{4,5},{6,7},{5,4},{7,6},{8,9},{10,11},{9,8... | collective-permute-start | bytes 1572872 | tf_op jit(solution)/shard_map/ppermute | solution.py:425
  6.0 11.8 %collective-permute-start.6 = (f32[512,128]{1,0:T(8,128)S(1)}, f32[512,128]{1,0:T(8,128)S(1)}, u32[]{:S(2)}, u32[]{:S(2)}) collective-permute-start(f32[512,128]{1,0:T(8,128)S(1)} %copy-done), channel_id=1, source_target_pairs={{0,4},{1,5},{2,6},{3,7},{8,12},{9,13},{10,14},{11,15},{4,0},{5,1},... | collective-permute-start | bytes 786440 | tf_op jit(solution)/shard_map/ppermute | solution.py:363
  6.4 11.4 %collective-permute-start.8 = (f32[512,128]{1,0:T(8,128)S(1)}, f32[512,128]{1,0:T(8,128)S(1)}, u32[]{:S(2)}, u32[]{:S(2)}) collective-permute-start(f32[512,128]{1,0:T(8,128)S(1)} %copy-done), channel_id=1, source_target_pairs={{4,8},{5,9},{6,10},{7,11},{8,4},{9,5},{10,6},{11,7},{0,1},{2,3},{1... | collective-permute-start | bytes 786440 | tf_op jit(solution)/shard_map/ppermute | solution.py:363
  16.3 12.1 %collective-permute-start.5 = (f32[1024,128]{1,0:T(8,128)S(1)}, f32[1024,128]{1,0:T(8,128)S(1)}, u32[]{:S(2)}, u32[]{:S(2)}) collective-permute-start(f32[1024,128]{1,0:T(8,128)S(1)} %collective-permute-done.4.refs_5_), channel_id=1, source_target_pairs={{3,2},{0,1},{2,3},{1,0},{7,6},{4,5},{6,7},{5,4},{11,10},{8,9},{10,... | collective-permute-start | bytes 1572872 | tf_op jit(solution)/shard_map/ppermute | solution.py:425
  16.3 3.9 %collective-permute-start.2 = (f32[512,128]{1,0:T(8,128)S(1)}, f32[512,128]{1,0:T(8,128)S(1)}, u32[]{:S(2)}, u32[]{:S(2)}) collective-permute-start(f32[512,128]{1,0:T(8,128)S(1)} %copy-done.1), channel_id=1, source_target_pairs={{4,8},{5,9},{6,10},{7,11},{8,4},{9,5},{10,6},{11,7},{0,1},{2,3},{1... | collective-permute-start | bytes 786440 | tf_op jit(solution)/shard_map/ppermute | solution.py:363
  17.8 7.5 %collective-permute-start.7 = (f32[512,128]{1,0:T(8,128)S(1)}, f32[512,128]{1,0:T(8,128)S(1)}, u32[]{:S(2)}, u32[]{:S(2)}) collective-permute-start(f32[512,128]{1,0:T(8,128)S(1)} %collective-permute-done.6.refs_2_), channel_id=1, source_target_pairs={{4,8},{5,9},{6,10},{7,11},{8,4},{9,5},{10,6},{11,7},{0,1},{2,3},{1... | collective-permute-start | bytes 786440 | tf_op jit(solution)/shard_map/ppermute | solution.py:363
  17.8 10.6 %collective-permute-start.9 = (f32[512,128]{1,0:T(8,128)S(1)}, f32[512,128]{1,0:T(8,128)S(1)}, u32[]{:S(2)}, u32[]{:S(2)}) collective-permute-start(f32[512,128]{1,0:T(8,128)S(1)} %collective-permute-done.8.refs_0_), channel_id=1, source_target_pairs={{8,12},{9,13},{10,14},{11,15},{4,0},{5,1},{6,2},{7,3},{24,28},{25,... | collective-permute-start | bytes 786440 | tf_op jit(solution)/shard_map/ppermute | solution.py:363
  20.2 9.9 %collective-permute-start.1 = (f32[512,128]{1,0:T(8,128)S(1)}, f32[512,128]{1,0:T(8,128)S(1)}, u32[]{:S(2)}, u32[]{:S(2)}) collective-permute-start(f32[512,128]{1,0:T(8,128)S(1)} %collective-permute-done.refs_3_), channel_id=1, source_target_pairs={{4,8},{5,9},{6,10},{7,11},{8,4},{9,5},{10,6},{11,7},{0,1},{2,3},{1... | collective-permute-start | bytes 786440 | tf_op jit(solution)/shard_map/ppermute | solution.py:363
  20.8 14.7 %collective-permute-start.3 = (f32[512,128]{1,0:T(8,128)S(1)}, f32[512,128]{1,0:T(8,128)S(1)}, u32[]{:S(2)}, u32[]{:S(2)}) collective-permute-start(f32[512,128]{1,0:T(8,128)S(1)} %collective-permute-done.2.refs_1_), channel_id=1, source_target_pairs={{8,12},{9,13},{10,14},{11,15},{4,0},{5,1},{6,2},{7,3},{24,28},{25,... | collective-permute-start | bytes 786440 | tf_op jit(solution)/shard_map/ppermute | solution.py:363
